TPU v7x, 32 devices: a whole 2x2x4 slice. The times are simulated.
32 devices in a mesh: seq: 8 (over y, x, core), head: 4 (over z).
Axes of the slice: x: 2, y: 2, z: 4, core: 2. Of those that a mesh axis runs over, the one named last changes fastest.
Arguments:
- query_rows: bfloat16 [8192, 2048], P(('seq', 'head')), may hold values from -1.796875 to 1.796875
- key_rows: bfloat16 [8192, 2048], P(('seq', 'head')), may hold values from -1.796875 to 1.796875
- value_rows: bfloat16 [8192, 2048], P(('seq', 'head')), may hold values from -1.796875 to 1.796875
- out_grad: bfloat16 [8192, 2048], P(('seq', 'head')), may hold values from -1.796875 to 1.796875
- decay: float32 [16, 8192], P('head', 'seq'), may hold values from 0 to 2
Outputs:
- attended: bfloat16 [8192, 2048], P(('seq', 'head'))
- query_grad: bfloat16 [8192, 2048], P(('seq', 'head'))
- key_grad: bfloat16 [8192, 2048], P(('seq', 'head'))
- value_grad: bfloat16 [8192, 2048], P(('seq', 'head'))
All inputs are finite; a program needn't handle non-finite values.
Results may differ from a plain program's by a relative error of at most 0.0083.
Values may be sent and summed in bfloat16 or wider, within the bound.
No kernel may reach another device: no remote copies, remote signals or barrier semaphores. Data moves between devices by JAX's collectives and lax.ppermute only.
A program may use at most 128 MiB of HBM per device.

v0:
```python
import functools

import jax
import jax.numpy as jnp
from jax import lax
from jax.experimental import pallas as pl
from jax.experimental.pallas import tpu as pltpu
from jax.sharding import PartitionSpec as P


SEQ = "seq"
HEAD = "head"
PAIR = 2
F32 = jnp.float32
BF16 = jnp.bfloat16


def dot(a, b, contract, precision=None):
    return lax.dot_general(
        a, b, (((contract[0],), (contract[1],)), ((), ())),
        precision=precision, preferred_element_type=F32,
    )


def params(mib=16):
    return pltpu.CompilerParams(vmem_limit_bytes=mib << 20)


def split(x):
    high = x.astype(BF16)
    rest = x - high.astype(F32)
    middle = rest.astype(BF16)
    return high, middle, (rest - middle.astype(F32)).astype(BF16)


def prepare(decay_refs, row_ref, col_ref):
    me = lax.axis_index(HEAD)
    owners = len(decay_refs)
    heads, tokens = row_ref.shape[1:]
    at = lax.broadcasted_iota(jnp.int32, (tokens, tokens), 0)
    by = lax.broadcasted_iota(jnp.int32, (tokens, tokens), 1)
    upto = (at <= by).astype(BF16)
    since = (by <= at).astype(BF16)
    start = pl.multiple_of(me * tokens, tokens)
    own = jnp.concatenate([ref[:, pl.ds(start, tokens)] for ref in decay_refs], axis=0)
    pieces = split(own)
    rows = sum(dot(piece, upto, (1, 0)) for piece in pieces)
    cols = sum(dot(since, piece, (1, 1)) for piece in pieces)
    for slot in range(owners):
        row_ref[slot] = rows[slot * heads : (slot + 1) * heads]
        col_ref[slot] = cols[:, slot * heads : (slot + 1) * heads]


def summarize(row_ref, columns_of, out_refs, low, part):
    _, tokens = row_ref.shape[1:]
    width = out_refs[0].shape[-1]
    scale = width ** (-0.5)
    for slot, out_ref in enumerate(out_refs):
        owner = lax.axis_index(HEAD) ^ slot
        row = row_ref[slot]
        weight = jnp.exp(-(row[:, tokens - 1 : tokens] - row))
        growth = jnp.exp(-row)
        for member in range(part):
            head = low + member
            q, k, v, g = columns_of(slot, owner, member)
            keyed = (k.T.astype(F32) * weight[head : head + 1]).astype(BF16)
            queried = (q.T.astype(F32) * growth[head : head + 1]).astype(BF16)
            out_ref[0, member] = dot(keyed, v, (1, 0)).astype(BF16)
            out_ref[1, member] = (scale * dot(queried, g, (1, 0))).astype(BF16)


def first_kernel(_, *refs, part, owners):
    decay_refs, refs = refs[:owners], refs[owners:]
    token_refs, refs = refs[:4], refs[4:]
    row_ref, col_ref, *out_refs, held, sems = refs
    heads = row_ref.shape[1]
    width = out_refs[0].shape[-1]
    copies = []
    for slot in range(owners):
        owner = lax.axis_index(HEAD) ^ slot
        cols = pl.ds(pl.multiple_of(owner * heads * width, width), part * width)
        copies.append(
            [
                pltpu.make_async_copy(ref.at[:, cols], held.at[index, slot], sems.at[index, slot])
                for index, ref in enumerate(token_refs)
            ]
        )
        for copy in copies[-1]:
            copy.start()
    prepare(decay_refs, row_ref, col_ref)

    def columns_of(slot, owner, member):
        if member == 0:
            for copy in copies[slot]:
                copy.wait()
        cols = slice(member * width, (member + 1) * width)
        return [held[index, slot, :, cols] for index in range(4)]

    summarize(row_ref, columns_of, out_refs, 0, part)


def later_kernel(row_ref, *refs, low, part):
    token_refs, out_refs = refs[:4], refs[4:]
    heads = row_ref.shape[1]
    width = out_refs[0].shape[-1]

    def columns_of(slot, owner, member):
        start = (owner * heads + low + member) * width
        return [ref[:, pl.ds(pl.multiple_of(start, width), width)] for ref in token_refs]

    summarize(row_ref, columns_of, out_refs, low, part)


def link_layout(owners):
    sizes = dict(near0=owners * owners, near1=owners * owners, after=owners, before=owners, block=1)
    at, total = {}, 0
    for name, size in sizes.items():
        at[name] = total
        total += size
    return sizes, at, -(-total // 8) * 8


def link_kernel(decay_ref, w_ref, *, owners):
    me = lax.axis_index(HEAD)
    sizes, at, length = link_layout(owners)
    heads = decay_ref.shape[0]
    tokens = decay_ref.shape[1] // owners
    index = lax.broadcasted_iota(jnp.int32, (length, 1), 0)
    low = high = keep = jnp.zeros((length, 1), jnp.int32)

    def put(name, low_, high_, keep_):
        nonlocal low, high, keep
        here = (index >= at[name]) & (index < at[name] + sizes[name])
        low = jnp.where(here, low_, low)
        high = jnp.where(here, high_, high)
        keep = jnp.where(here, jnp.where(keep_, 1, 0), keep)

    for side in range(2):
        r = index - at[f"near{side}"]
        to = me ^ lax.div(r, owners)
        of = me ^ lax.rem(r, owners)
        if side == 0:
            put("near0", of, to, of < to)
        else:
            put("near1", to, of, to < of)
    put("after", me ^ (index - at["after"]), owners, index >= 0)
    put("before", -1, me ^ (index - at["before"]), index >= 0)
    put("block", -1, owners, index >= 0)
    spot = lax.broadcasted_iota(jnp.int32, (length, owners * tokens), 1)
    inside = ((spot >= (low + 1) * tokens) & (spot < high * tokens)).astype(BF16)
    total = sum(dot(inside, piece, (1, 1)) for piece in split(decay_ref[...]))
    weight = jnp.where(keep > 0, jnp.exp(-total), 0.0)
    weight = jnp.where(index == at["block"], total, weight)
    for head in range(heads):
        w_ref[head] = jnp.broadcast_to(weight[:, head : head + 1], w_ref.shape[1:])


def extra_rows(part):
    return -(-3 * part // 16) * 16


def log_rows(logs):
    part, lanes = logs.shape
    rows = [piece.astype(F32) for piece in split(logs)]
    rows.append(jnp.zeros((extra_rows(part) - 3 * part, lanes), F32))
    return jnp.concatenate(rows, axis=0).astype(BF16)


def get_logs(ref, part):
    rows = ref[ref.shape[0] - extra_rows(part) :].astype(F32)
    return rows[:part] + rows[part : 2 * part] + rows[2 * part : 3 * part]


def total_kernel(w_ref, *refs, low, part, at, owners):
    out_ref = refs[-1]
    width = out_ref.shape[1]
    for side, name in enumerate(("after", "before")):
        for member in range(part):
            total = 0.0
            for slot, ref in enumerate(refs[:owners]):
                index = at[name] + slot
                total = total + w_ref[low + member, index : index + 1] * ref[side, member].astype(F32)
            rows = slice((side * part + member) * width, (side * part + member + 1) * width)
            out_ref[rows] = total.astype(BF16)
    index = at["block"]
    logs = jnp.concatenate([w_ref[low + m, index : index + 1] for m in range(part)], axis=0)
    out_ref[2 * part * width :] = log_rows(logs)


def pair_kernel(own_ref, other_ref, *out_refs, part):
    far_at = lax.div(lax.axis_index(SEQ), PAIR)
    lead = lax.rem(lax.axis_index(SEQ), PAIR) == 0
    width = own_ref.shape[1]
    own_logs, other_logs = get_logs(own_ref, part), get_logs(other_ref, part)
    over_own, over_other = jnp.exp(-own_logs), jnp.exp(-other_logs)
    weights = (
        (jnp.where(lead, over_other, 1.0), jnp.where(lead, 1.0, over_own)),
        (jnp.where(lead, 1.0, over_other), jnp.where(lead, over_own, 1.0)),
    )
    both_logs = log_rows(own_logs + other_logs)
    for member in range(part):
        both = []
        for side, (own, other) in enumerate(weights):
            rows = slice((side * part + member) * width, (side * part + member + 1) * width)
            both.append(
                own[member : member + 1] * own_ref[rows].astype(F32)
                + other[member : member + 1] * other_ref[rows].astype(F32)
            )
        both = [value.astype(BF16) for value in both]
        for slot, out_ref in enumerate(out_refs):
            onward = (far_at ^ (slot + 1)) > far_at
            rows = slice(member * width, (member + 1) * width)
            out_ref[rows] = jnp.where(onward, both[0], both[1])
    for out_ref in out_refs:
        out_ref[part * width :] = both_logs


def state_kernel(w_ref, *refs, low, part, at, owners, far):
    far_at = lax.div(lax.axis_index(SEQ), PAIR)
    lead = lax.rem(lax.axis_index(SEQ), PAIR) == 0
    ins = refs[:owners]
    other_ref = refs[owners]
    far_refs = refs[owners + 1 : owners + 1 + far]
    out_refs = refs[owners + 1 + far :]
    width = other_ref.shape[1]
    other_logs = get_logs(other_ref, part)
    far_logs = [get_logs(ref, part) for ref in far_refs]
    sources = [far_at ^ (slot + 1) for slot in range(far)]
    for side, enter in enumerate(("before", "after")):
        here = lead if side == 1 else jnp.logical_not(lead)
        gone = jnp.where(here, other_logs, 0.0)
        factors = []
        for source in sources:
            use = source < far_at if side == 0 else source > far_at
            log = gone
            for between, logs in zip(sources, far_logs):
                if side == 0:
                    inside = (between > source) & (between < far_at)
                else:
                    inside = (between < source) & (between > far_at)
                log = log + jnp.where(inside, logs, 0.0)
            factors.append(jnp.where(use, jnp.exp(-log), 0.0))
        for member in range(part):
            rows = slice((side * part + member) * width, (side * part + member + 1) * width)
            base = jnp.where(here, other_ref[rows].astype(F32), 0.0)
            rows = slice(member * width, (member + 1) * width)
            for factor, ref in zip(factors, far_refs):
                base = base + factor[member : member + 1] * ref[rows].astype(F32)
            pieces = [ref[side, member].astype(F32) for ref in ins]
            for slot, out_ref in enumerate(out_refs):
                index = at[enter] + slot
                value = w_ref[low + member, index : index + 1] * base
                for source, piece in enumerate(pieces):
                    if source != slot:
                        index = at[f"near{side}"] + slot * owners + source
                        value = value + w_ref[low + member, index : index + 1] * piece
                out_ref[side, member] = value.astype(BF16)


def inner_parts(row, col, q, k, v, g):
    tokens, width = q.shape
    scale = width ** (-0.5)
    at = lax.broadcasted_iota(jnp.int32, (tokens, tokens), 0)
    by = lax.broadcasted_iota(jnp.int32, (tokens, tokens), 1)
    causal = at >= by
    mask = jnp.where(causal, scale * jnp.exp(-jnp.where(causal, col - row, 0.0)), 0.0)
    scores = (dot(q, k, (1, 1)) * mask).astype(BF16)
    grads = (dot(g, v, (1, 1)) * mask).astype(BF16)
    return (
        dot(scores, v, (1, 0)),
        dot(grads, k, (1, 0)),
        dot(grads, q, (0, 0)),
        dot(scores, g, (0, 0)),
    )


def inner_kernel(row_ref, col_ref, q_ref, k_ref, v_ref, g_ref, *refs, low, part, owners):
    part_refs, scaled_refs = refs[:4], refs[4:]
    heads, tokens = row_ref.shape[1:]
    width = part_refs[0].shape[2] // part
    scale = width ** (-0.5)
    for slot in range(owners):
        owner = lax.axis_index(HEAD) ^ slot
        for member in range(part):
            head = low + member
            cols = pl.ds(pl.multiple_of((owner * heads + head) * width, width), width)
            here = slice(member * width, (member + 1) * width)
            row = row_ref[slot][head : head + 1, :]
            col = col_ref[slot][:, head : head + 1]
            weight = jnp.exp(-(row[:, tokens - 1 : tokens] - col))
            growth = scale * jnp.exp(-col)
            q, k, v, g = q_ref[:, cols], k_ref[:, cols], v_ref[:, cols], g_ref[:, cols]
            for ref, value in zip(part_refs, inner_parts(row, col, q, k, v, g)):
                ref[slot, :, here] = value
            for ref, rows, factor in zip(scaled_refs, (q, g, v, k), (growth, growth, weight, weight)):
                ref[slot, :, here] = (rows.astype(F32) * factor).astype(BF16)


def result_kernel(*refs, low, part, owners, slots, carried):
    state_refs, refs = refs[: len(slots)], refs[len(slots) :]
    part_refs, scaled_refs, refs = refs[:4], refs[4:8], refs[8 + carried :]
    out_refs, held, sems = refs[:4], *refs[4:]
    width = held.shape[3] // part
    heads = out_refs[0].shape[1] // (owners * width)
    copies = []
    for slot, state_ref in zip(slots, state_refs):
        for member in range(part):
            here = slice(member * width, (member + 1) * width)
            for index in range(4):
                state = state_ref[index // 2, member]
                turned = index in (1, 2)
                value = dot(scaled_refs[index][slot, :, here], state, (1, 1 if turned else 0))
                held[index, slot, :, here] = (part_refs[index][slot, :, here] + value).astype(BF16)
        start = ((lax.axis_index(HEAD) ^ slot) * heads + low) * width
        cols = pl.ds(pl.multiple_of(start, width), part * width)
        for index, out_ref in enumerate(out_refs):
            copy = pltpu.make_async_copy(
                held.at[index, slot], out_ref.at[:, cols], sems.at[index, slot]
            )
            copy.start()
            copies.append(copy)
    for copy in copies:
        copy.wait()


def chunk_sizes(heads):
    return [heads - heads // 2, heads // 2] if heads >= 2 else [heads]


def on_device(query_rows, key_rows, value_rows, out_grad, decay, *, seq_size, owners):
    heads = decay.shape[0]
    tokens, columns = query_rows.shape
    width = columns // (heads * owners)
    chunks = chunk_sizes(heads)
    chunks = [(sum(chunks[:i]), part) for i, part in enumerate(chunks)]
    far = seq_size // PAIR - 1
    _, at, table = link_layout(owners)

    def swap(array, axis, size, offset):
        return lax.ppermute(array, axis, [(i, i ^ offset) for i in range(size)])

    def exchange(arrays):
        return [arrays[0]] + [swap(arrays[slot], HEAD, owners, slot) for slot in range(1, owners)]

    whole = pl.BlockSpec(memory_space=pltpu.VMEM)
    row_shape = jax.ShapeDtypeStruct((owners, heads, tokens), F32)
    col_shape = jax.ShapeDtypeStruct((owners, tokens, heads), F32)
    inputs = (query_rows, key_rows, value_rows, out_grad)

    def state_shapes(part):
        return (jax.ShapeDtypeStruct((2, part, width, width), BF16),) * owners

    def cost(flops, passes, part):
        share = tokens * owners * part * width
        return pl.CostEstimate(flops=flops * share, bytes_accessed=2 * passes * share, transcendentals=0)

    decays = exchange([decay] * owners)
    hbm = pl.BlockSpec(memory_space=pltpu.HBM)
    anywhere = pl.BlockSpec(memory_space=pl.ANY)
    weights = pl.pallas_call(
        functools.partial(link_kernel, owners=owners),
        out_shape=jax.ShapeDtypeStruct((heads, table, width), F32),
        in_specs=[whole],
        out_specs=whole,
        cost_estimate=pl.CostEstimate(flops=0, bytes_accessed=24 * tokens * columns, transcendentals=0),
        compiler_params=params(),
        name="link",
    )(decay)
    part = chunks[0][1]
    rows, cols, *first = pl.pallas_call(
        functools.partial(first_kernel, part=part, owners=owners),
        out_shape=(row_shape, col_shape) + state_shapes(part),
        in_specs=[anywhere] + [whole] * owners + [hbm] * 4,
        out_specs=(whole,) * (2 + owners),
        scratch_shapes=[
            pltpu.VMEM((4, owners, tokens, part * width), BF16),
            pltpu.SemaphoreType.DMA((4, owners)),
        ],
        cost_estimate=cost(4 * width, 4, part),
        compiler_params=params(),
        name="first",
    )(weights, *decays, *[pltpu.with_memory_space_constraint(x, pltpu.HBM) for x in inputs])
    summaries = [first]
    for low, part in chunks[1:]:
        summary_call = pl.pallas_call(
            functools.partial(later_kernel, low=low, part=part),
            out_shape=state_shapes(part),
            in_specs=[whole] * 5,
            out_specs=(whole,) * owners,
            cost_estimate=cost(4 * width, 4, part),
            compiler_params=params(),
        )
        summaries.append(summary_call(rows, *inputs))

    outs = None
    for chunk, (low, part) in enumerate(chunks):
        total_shape = jax.ShapeDtypeStruct((2 * part * width + extra_rows(part), width), BF16)
        far_shape = jax.ShapeDtypeStruct((part * width + extra_rows(part), width), BF16)
        part_shape = jax.ShapeDtypeStruct((owners, tokens, part * width), F32)
        scaled_shape = jax.ShapeDtypeStruct((owners, tokens, part * width), BF16)
        own = summaries[chunk]
        here = exchange(own)
        total_call = pl.pallas_call(
            functools.partial(total_kernel, low=low, part=part, at=at, owners=owners),
            out_shape=total_shape,
            in_specs=[whole] * (owners + 1),
            out_specs=whole,
            compiler_params=params(),
        )
        total = total_call(weights, *here)
        other = swap(total, SEQ, seq_size, 1)
        sent = pl.pallas_call(
            functools.partial(pair_kernel, part=part),
            out_shape=(far_shape,) * far,
            in_specs=[whole, whole],
            out_specs=(whole,) * far,
            compiler_params=params(),
        )(total, other)
        heard = [swap(array, SEQ, seq_size, PAIR * (slot + 1)) for slot, array in enumerate(sent)]
        state_call = pl.pallas_call(
            functools.partial(
                state_kernel, low=low, part=part, at=at, owners=owners, far=far
            ),
            out_shape=state_shapes(part),
            in_specs=[whole] * (owners + far + 2),
            out_specs=(whole,) * owners,
            compiler_params=params(),
        )
        states = state_call(weights, *here, other, *heard)
        states = exchange(states)
        inner_call = pl.pallas_call(
            functools.partial(inner_kernel, low=low, part=part, owners=owners),
            out_shape=(part_shape,) * 4 + (scaled_shape,) * 4,
            in_specs=[whole] * 6,
            out_specs=(whole,) * 8,
            cost_estimate=cost(12 * tokens, 12, part),
            compiler_params=params(),
        )
        parts = inner_call(rows, cols, *inputs)
        for slots in (range(1), range(1, owners)) if chunk == len(chunks) - 1 else (range(owners),):
            carried = 0 if outs is None else 4
            first_carried = 8 + len(slots)
            outs = pl.pallas_call(
                functools.partial(
                    result_kernel,
                    low=low,
                    part=part,
                    owners=owners,
                    slots=tuple(slots),
                    carried=carried,
                ),
                out_shape=(jax.ShapeDtypeStruct((tokens, columns), BF16),) * 4,
                in_specs=[whole] * (8 + len(slots)) + [hbm] * carried,
                out_specs=(hbm,) * 4,
                scratch_shapes=[
                    pltpu.VMEM((4, owners, tokens, part * width), BF16),
                    pltpu.SemaphoreType.DMA((4, owners)),
                ],
                input_output_aliases={first_carried + i: i for i in range(carried)},
                cost_estimate=cost(8 * width, 8, part),
                compiler_params=params(),
            )(*[states[slot] for slot in slots], *parts, *(outs or ()))
    return tuple(outs)


def solution(mesh):
    spec = P((SEQ, HEAD), None)

    def body(*args):
        return on_device(*args, seq_size=mesh.shape[SEQ], owners=mesh.shape[HEAD])

    return jax.shard_map(
        body,
        mesh=mesh,
        in_specs=(spec, spec, spec, spec, P(HEAD, SEQ)),
        out_specs=(spec, spec, spec, spec),
        check_vma=False,
    )
```

profile of v0, /device:TPU:0, one launch (start us, length us, event | category | flops | bytes accessed | tf_op | source)
XLA Modules:
  0.0 74.9 jit_solution(12054237583226428400)
XLA Ops:
  0.6 4.1 %collective-permute-start.1 = (f32[4,1024]{1,0:T(4,128)}, f32[4,1024]{1,0:T(4,128)S(1)}, u32[]{:S(2)}, u32[]{:S(2)}) collective-permute-start(f32[4,1024]{1,0:T(4,128)} %refs_0_.2), channel_id=1, source_target_pairs={{0,2},{1,3},{2,0},{3,1},{4,6},{5,7},{6,4},{7,5},{8,10},{9,11},{10,... | collective-permute-start | bytes 49160 | tf_op jit(solution)/shard_map/ppermute | solution.py:340
  4.8 1.6 %collective-permute-start = (f32[4,1024]{1,0:T(4,128)}, f32[4,1024]{1,0:T(4,128)S(1)}, u32[]{:S(2)}, u32[]{:S(2)}) collective-permute-start(f32[4,1024]{1,0:T(4,128)} %refs_0_.2), channel_id=1, source_target_pairs={{0,1},{1,0},{2,3},{3,2},{4,5},{5,4},{6,7},{7,6},{8,9},{9,8},{10,11... | collective-permute-start | bytes 49160 | tf_op jit(solution)/shard_map/ppermute | solution.py:340
  6.3 0.0 collective-permute-start.2
  6.3 0.8 %copy-done.4 = f32[4,1024]{1,0:T(4,128)S(1)} copy-done((f32[4,1024]{1,0:T(4,128)S(1)}, f32[4,1024]{1,0:T(4,128)}, u32[]{:S(2)}) %copy-start.4) | copy-done | bytes 16408
  7.1 0.3 link.1._.w_ref
  7.4 0.0 copy-start
  7.5 0.0 copy-start.1
  7.5 0.0 copy-start.2
  7.5 0.0 copy-start.3
  7.5 0.0 collective-permute-done.1.refs_2_
  7.5 1.2 %collective-permute-done.refs_1_ = f32[4,1024]{1,0:T(4,128)S(1)} collective-permute-done((f32[4,1024]{1,0:T(4,128)}, f32[4,1024]{1,0:T(4,128)S(1)}, u32[]{:S(2)}, u32[]{:S(2)}) %collective-permute-start) | collective-permute-done | bytes 16416 | tf_op jit(solution)/shard_map/ppermute | solution.py:340
  8.7 3.4 %collective-permute-done.2.refs_3_ = f32[4,1024]{1,0:T(4,128)S(1)} collective-permute-done((f32[4,1024]{1,0:T(4,128)}, f32[4,1024]{1,0:T(4,128)S(1)}, u32[]{:S(2)}, u32[]{:S(2)}) %collective-permute-start.2) | collective-permute-done | bytes 16416 | tf_op jit(solution)/shard_map/ppermute | solution.py:340
  12.1 2.4 %first.1 = (f32[4,4,256]{2,1,0:T(4,128)S(1)}, f32[4,256,4]{2,1,0:T(8,128)S(1)}, bf16[2,2,128,128]{3,2,1,0:T(8,128)(2,1)S(1)}, bf16[2,2,128,128]{3,2,1,0:T(8,128)...) custom-call(f32[4,48,128]{2,1,0:T(8,128)S(1)} %link.1._.w_ref, ...), custom_call_target="tpu_custom_call" | custom-call | flops 134217728 | bytes 2097152 | tf_op jit(solution)/shard_map/first/pallas_call | solution.py:370
  14.5 0.1 collective-permute-start.13
  14.6 0.9 %collective-permute-start.14 = (bf16[2,2,128,128]{3,2,1,0:T(8,128)(2,1)S(1)}, bf16[2,2,128,128]{3,2,1,0:T(8,128)(2,1)S(1)}, u32[]{:S(2)}, u32[]{:S(2)}) collective-permute-start(bf16[2,2,128,128]{3,2,1,0:T(8,128)(2,1)S(1)} %get-tuple-element.75), channel_id=1, source_target_pairs={{0,2},{1,3},{2,0},{3,1},{4,6},{5,7},{6,4},{7,5},{8,10},{9,11},{10,... | collective-permute-start | bytes 393224 | tf_op jit(solution)/shard_map/ppermute | solution.py:340
  15.5 3.5 %collective-permute-start.15 = (bf16[2,2,128,128]{3,2,1,0:T(8,128)(2,1)S(1)}, bf16[2,2,128,128]{3,2,1,0:T(8,128)(2,1)S(1)}, u32[]{:S(2)}, u32[]{:S(2)}) collective-permute-start(bf16[2,2,128,128]{3,2,1,0:T(8,128)(2,1)S(1)} %get-tuple-element.76), channel_id=1, source_target_pairs={{0,3},{1,2},{2,1},{3,0},{4,7},{5,6},{6,5},{7,4},{8,11},{9,10},{10,... | collective-permute-start | bytes 393224 | tf_op jit(solution)/shard_map/ppermute | solution.py:340
  19.0 0.8 %shard_map.84 = (bf16[2,2,128,128]{3,2,1,0:T(8,128)(2,1)S(1)}, bf16[2,2,128,128]{3,2,1,0:T(8,128)(2,1)S(1)}, bf16[2,2,128,128]{3,2,1,0:T(8,128)(2,1)S(1)}, bf16[2,2,128,128]{3,2,1,0:T(8,128)(2,1)S(1)}) custom-call(f32[4,4,256]{2,1,0:T(4,128)S(1)} %get-tuple-element.52.row_ref, bf16[256,2048]{1,0:T(8,128)(2,1)S(1)} %copy-done, ...), custom_call_target="tpu_custom_call" | custom-call | flops 134217728 | bytes 2097152 | tf_op jit(solution)/shard_map/pallas_call | solution.py:393
  19.8 0.1 collective-permute-start.3
  19.9 0.9 %collective-permute-start.4 = (bf16[2,2,128,128]{3,2,1,0:T(8,128)(2,1)S(1)}, bf16[2,2,128,128]{3,2,1,0:T(8,128)(2,1)S(1)}, u32[]{:S(2)}, u32[]{:S(2)}) collective-permute-start(bf16[2,2,128,128]{3,2,1,0:T(8,128)(2,1)S(1)} %get-tuple-element.55), channel_id=1, source_target_pairs={{0,2},{1,3},{2,0},{3,1},{4,6},{5,7},{6,4},{7,5},{8,10},{9,11},{10,... | collective-permute-start | bytes 393224 | tf_op jit(solution)/shard_map/ppermute | solution.py:340
  20.8 0.1 collective-permute-done.13.refs_1_
  20.9 3.3 %collective-permute-start.5 = (bf16[2,2,128,128]{3,2,1,0:T(8,128)(2,1)S(1)}, bf16[2,2,128,128]{3,2,1,0:T(8,128)(2,1)S(1)}, u32[]{:S(2)}, u32[]{:S(2)}) collective-permute-start(bf16[2,2,128,128]{3,2,1,0:T(8,128)(2,1)S(1)} %get-tuple-element.56), channel_id=1, source_target_pairs={{0,3},{1,2},{2,1},{3,0},{4,7},{5,6},{6,5},{7,4},{8,11},{9,10},{10,... | collective-permute-start | bytes 393224 | tf_op jit(solution)/shard_map/ppermute | solution.py:340
  24.3 7.8 %collective-permute-done.14.refs_2_ = bf16[2,2,128,128]{3,2,1,0:T(8,128)(2,1)S(1)} collective-permute-done((bf16[2,2,128,128]{3,2,1,0:T(8,128)(2,1)S(1)}, bf16[2,2,128,128]{3,2,1,0:T(8,128)(2,1)S(1)}, u32[]{:S(2)}, u32[]{:S(2)}) %collective-permute-start.14) | collective-permute-done | bytes 131104 | tf_op jit(solution)/shard_map/ppermute | solution.py:340
  32.1 0.0 collective-permute-done.15.refs_3_
  32.1 0.1 shard_map.89.own_ref
  32.2 0.1 collective-permute-start.16
  32.3 0.0 collective-permute-done.3.refs_1_
  32.3 5.2 %collective-permute-done.4.refs_2_ = bf16[2,2,128,128]{3,2,1,0:T(8,128)(2,1)S(1)} collective-permute-done((bf16[2,2,128,128]{3,2,1,0:T(8,128)(2,1)S(1)}, bf16[2,2,128,128]{3,2,1,0:T(8,128)(2,1)S(1)}, u32[]{:S(2)}, u32[]{:S(2)}) %collective-permute-start.4) | collective-permute-done | bytes 131104 | tf_op jit(solution)/shard_map/ppermute | solution.py:340
  37.4 0.0 collective-permute-done.5.refs_3_
  37.4 0.1 shard_map.85.own_ref
  37.6 0.1 collective-permute-start.6
  37.6 0.0 collective-permute-done.16.other_ref.refs_4_
  37.6 0.1 shard_map.90
  37.8 1.6 %collective-permute-start.17 = (bf16[272,128]{1,0:T(8,128)(2,1)S(1)}, bf16[272,128]{1,0:T(8,128)(2,1)S(1)}, u32[]{:S(2)}, u32[]{:S(2)}) collective-permute-start(bf16[272,128]{1,0:T(8,128)(2,1)S(1)} %get-tuple-element.77), channel_id=1, source_target_pairs={{0,8},{4,12},{8,0},{12,4},{16,24},{20,28},{24,16},{28,20},{1,9},{5... | collective-permute-start | bytes 208904 | tf_op jit(solution)/shard_map/ppermute | solution.py:340
  39.3 1.5 %collective-permute-start.18 = (bf16[272,128]{1,0:T(8,128)(2,1)S(1)}, bf16[272,128]{1,0:T(8,128)(2,1)S(1)}, u32[]{:S(2)}, u32[]{:S(2)}) collective-permute-start(bf16[272,128]{1,0:T(8,128)(2,1)S(1)} %get-tuple-element.78), channel_id=1, source_target_pairs={{0,16},{4,20},{8,24},{12,28},{16,0},{20,4},{24,8},{28,12},{1,17},{... | collective-permute-start | bytes 208904 | tf_op jit(solution)/shard_map/ppermute | solution.py:340
  40.8 0.5 collective-permute-start.19
  41.3 1.1 %collective-permute-done.17.refs_5_ = bf16[272,128]{1,0:T(8,128)(2,1)S(1)} collective-permute-done((bf16[272,128]{1,0:T(8,128)(2,1)S(1)}, bf16[272,128]{1,0:T(8,128)(2,1)S(1)}, u32[]{:S(2)}, u32[]{:S(2)}) %collective-permute-start.17) | collective-permute-done | bytes 69664 | tf_op jit(solution)/shard_map/ppermute | solution.py:340
  42.4 1.2 %collective-permute-done.18.refs_6_ = bf16[272,128]{1,0:T(8,128)(2,1)S(1)} collective-permute-done((bf16[272,128]{1,0:T(8,128)(2,1)S(1)}, bf16[272,128]{1,0:T(8,128)(2,1)S(1)}, u32[]{:S(2)}, u32[]{:S(2)}) %collective-permute-start.18) | collective-permute-done | bytes 69664 | tf_op jit(solution)/shard_map/ppermute | solution.py:340
  43.6 2.4 %collective-permute-done.19.refs_7_ = bf16[272,128]{1,0:T(8,128)(2,1)S(1)} collective-permute-done((bf16[272,128]{1,0:T(8,128)(2,1)S(1)}, bf16[272,128]{1,0:T(8,128)(2,1)S(1)}, u32[]{:S(2)}, u32[]{:S(2)}) %collective-permute-start.19) | collective-permute-done | bytes 69664 | tf_op jit(solution)/shard_map/ppermute | solution.py:340
  46.0 0.4 shard_map.91
  46.4 2.0 %collective-permute-start.20 = (bf16[2,2,128,128]{3,2,1,0:T(8,128)(2,1)S(1)}, bf16[2,2,128,128]{3,2,1,0:T(8,128)(2,1)S(1)}, u32[]{:S(2)}, u32[]{:S(2)}) collective-permute-start(bf16[2,2,128,128]{3,2,1,0:T(8,128)(2,1)S(1)} %get-tuple-element.81), channel_id=1, source_target_pairs={{0,1},{1,0},{2,3},{3,2},{4,5},{5,4},{6,7},{7,6},{8,9},{9,8},{10,11... | collective-permute-start | bytes 393224 | tf_op jit(solution)/shard_map/ppermute | solution.py:340
  48.5 0.0 collective-permute-done.6.other_ref.refs_4_
  48.5 0.1 shard_map.86
  48.6 0.6 collective-permute-start.7
  49.2 0.6 collective-permute-start.8
  49.8 2.4 %collective-permute-start.9 = (bf16[272,128]{1,0:T(8,128)(2,1)S(1)}, bf16[272,128]{1,0:T(8,128)(2,1)S(1)}, u32[]{:S(2)}, u32[]{:S(2)}) collective-permute-start(bf16[272,128]{1,0:T(8,128)(2,1)S(1)} %get-tuple-element.59), channel_id=1, source_target_pairs={{0,24},{4,28},{8,16},{12,20},{16,8},{20,12},{24,0},{28,4},{1,25},{... | collective-permute-start | bytes 208904 | tf_op jit(solution)/shard_map/ppermute | solution.py:340
  52.1 0.0 collective-permute-start.21
  52.1 0.8 %collective-permute-done.7.refs_5_ = bf16[272,128]{1,0:T(8,128)(2,1)S(1)} collective-permute-done((bf16[272,128]{1,0:T(8,128)(2,1)S(1)}, bf16[272,128]{1,0:T(8,128)(2,1)S(1)}, u32[]{:S(2)}, u32[]{:S(2)}) %collective-permute-start.7) | collective-permute-done | bytes 69664 | tf_op jit(solution)/shard_map/ppermute | solution.py:340
  53.0 1.6 %collective-permute-start.22 = (bf16[2,2,128,128]{3,2,1,0:T(8,128)(2,1)S(1)}, bf16[2,2,128,128]{3,2,1,0:T(8,128)(2,1)S(1)}, u32[]{:S(2)}, u32[]{:S(2)}) collective-permute-start(bf16[2,2,128,128]{3,2,1,0:T(8,128)(2,1)S(1)} %get-tuple-element.83), channel_id=1, source_target_pairs={{0,3},{1,2},{2,1},{3,0},{4,7},{5,6},{6,5},{7,4},{8,11},{9,10},{10,... | collective-permute-start | bytes 393224 | tf_op jit(solution)/shard_map/ppermute | solution.py:340
  54.6 0.0 collective-permute-done.8.refs_6_
  54.6 0.4 collective-permute-done.9.refs_7_
  55.0 0.4 shard_map.87
  55.4 0.7 collective-permute-start.10
  56.1 1.7 %collective-permute-start.11 = (bf16[2,2,128,128]{3,2,1,0:T(8,128)(2,1)S(1)}, bf16[2,2,128,128]{3,2,1,0:T(8,128)(2,1)S(1)}, u32[]{:S(2)}, u32[]{:S(2)}) collective-permute-start(bf16[2,2,128,128]{3,2,1,0:T(8,128)(2,1)S(1)} %get-tuple-element.61), channel_id=1, source_target_pairs={{0,2},{1,3},{2,0},{3,1},{4,6},{5,7},{6,4},{7,5},{8,10},{9,11},{10,... | collective-permute-start | bytes 393224 | tf_op jit(solution)/shard_map/ppermute | solution.py:340
  57.8 0.0 collective-permute-done.20.refs_1_
  57.8 2.0 %collective-permute-start.12 = (bf16[2,2,128,128]{3,2,1,0:T(8,128)(2,1)S(1)}, bf16[2,2,128,128]{3,2,1,0:T(8,128)(2,1)S(1)}, u32[]{:S(2)}, u32[]{:S(2)}) collective-permute-start(bf16[2,2,128,128]{3,2,1,0:T(8,128)(2,1)S(1)} %get-tuple-element.62), channel_id=1, source_target_pairs={{0,3},{1,2},{2,1},{3,0},{4,7},{5,6},{6,5},{7,4},{8,11},{9,10},{10,... | collective-permute-start | bytes 393224 | tf_op jit(solution)/shard_map/ppermute | solution.py:340
  59.9 3.0 %shard_map.92 = (f32[4,256,256]{2,1,0:T(8,128)S(1)}, f32[4,256,256]{2,1,0:T(8,128)S(1)}, f32[4,256,256]{2,1,0:T(8,128)S(1)}, f32[4,256,256]{2,1,0:T(8,128)S(1)},...) custom-call(f32[4,4,256]{2,1,0:T(4,128)S(1)} %get-tuple-element.52.r, ...), custom_call_target="tpu_custom_call" | custom-call | flops 805306368 | bytes 6291456 | tf_op jit(solution)/shard_map/pallas_call | solution.py:439
  62.9 3.0 %shard_map.88 = (f32[4,256,256]{2,1,0:T(8,128)S(1)}, f32[4,256,256]{2,1,0:T(8,128)S(1)}, f32[4,256,256]{2,1,0:T(8,128)S(1)}, f32[4,256,256]{2,1,0:T(8,128)S(1)},...) custom-call(f32[4,4,256]{2,1,0:T(4,128)S(1)} %get-tuple-element.52.r, ...), custom_call_target="tpu_custom_call" | custom-call | flops 805306368 | bytes 6291456 | tf_op jit(solution)/shard_map/pallas_call | solution.py:439
  65.9 1.8 %collective-permute-done.21.refs_2_ = bf16[2,2,128,128]{3,2,1,0:T(8,128)(2,1)S(1)} collective-permute-done((bf16[2,2,128,128]{3,2,1,0:T(8,128)(2,1)S(1)}, bf16[2,2,128,128]{3,2,1,0:T(8,128)(2,1)S(1)}, u32[]{:S(2)}, u32[]{:S(2)}) %collective-permute-start.21) | collective-permute-done | bytes 131104 | tf_op jit(solution)/shard_map/ppermute | solution.py:340
  67.7 0.0 collective-permute-done.22.refs_3_
  67.7 1.7 %shard_map.93 = (bf16[256,2048]{1,0:T(8,128)(2,1)}, bf16[256,2048]{1,0:T(8,128)(2,1)}, bf16[256,2048]{1,0:T(8,128)(2,1)}, bf16[256,2048]{1,0:T(8,128)(2,1)}) custom-call(bf16[2,2,128,128]{3,2,1,0:T(8,128)(2,1)S(1)} %get-tuple-element.80.refs_0_, bf16[2,2,128,128]{3,2,1,0:T(8,128)(2,1)S(1)} %collective-permute-done.20.refs_1_, ...), custom_call_target="tpu_custom_call" | custom-call | flops 268435456 | bytes 4194304 | tf_op jit(solution)/shard_map/pallas_call | solution.py:443
  69.5 1.2 %shard_map.94 = (bf16[256,2048]{1,0:T(8,128)(2,1)}, bf16[256,2048]{1,0:T(8,128)(2,1)}, bf16[256,2048]{1,0:T(8,128)(2,1)}, bf16[256,2048]{1,0:T(8,128)(2,1)}) custom-call(bf16[2,2,128,128]{3,2,1,0:T(8,128)(2,1)S(1)} %get-tuple-element.72.refs_0_, ...), custom_call_target="tpu_custom_call", output_to_operand_aliasing={{0}: (9, {}), {1}: (10, {}), {2}: (11, {}), {3}: (12, {})} | custom-call | flops 268435456 | bytes 4194304 | tf_op jit(solution)/shard_map/pallas_call | solution.py:443
  70.7 0.0 collective-permute-done.10.refs_0_
  70.7 2.6 %collective-permute-done.11.refs_1_ = bf16[2,2,128,128]{3,2,1,0:T(8,128)(2,1)S(1)} collective-permute-done((bf16[2,2,128,128]{3,2,1,0:T(8,128)(2,1)S(1)}, bf16[2,2,128,128]{3,2,1,0:T(8,128)(2,1)S(1)}, u32[]{:S(2)}, u32[]{:S(2)}) %collective-permute-start.11) | collective-permute-done | bytes 131104 | tf_op jit(solution)/shard_map/ppermute | solution.py:340
  73.3 1.6 %shard_map.95 = (bf16[256,2048]{1,0:T(8,128)(2,1)}, bf16[256,2048]{1,0:T(8,128)(2,1)}, bf16[256,2048]{1,0:T(8,128)(2,1)}, bf16[256,2048]{1,0:T(8,128)(2,1)}) custom-call(bf16[2,2,128,128]{3,2,1,0:T(8,128)(2,1)S(1)} %collective-permute-done.10.refs_0_, ...), custom_call_target="tpu_custom_call", output_to_operand_aliasing={{0}: (11, {}), {1}: (12, {}), {2}: (13, {}), {3}: (14, {})} | custom-call | flops 268435456 | bytes 4194304 | tf_op jit(solution)/shard_map/pallas_call | solution.py:443
  (6 shorter events, 0.0 us)
Async XLA Ops:
  0.6 6.9 %collective-permute-start.1 = (f32[4,1024]{1,0:T(4,128)}, f32[4,1024]{1,0:T(4,128)S(1)}, u32[]{:S(2)}, u32[]{:S(2)}) collective-permute-start(f32[4,1024]{1,0:T(4,128)} %refs_0_.2), channel_id=1, source_target_pairs={{0,2},{1,3},{2,0},{3,1},{4,6},{5,7},{6,4},{7,5},{8,10},{9,11},{10,... | collective-permute-start | bytes 49160 | tf_op jit(solution)/shard_map/ppermute | solution.py:340
  4.8 3.9 %collective-permute-start = (f32[4,1024]{1,0:T(4,128)}, f32[4,1024]{1,0:T(4,128)S(1)}, u32[]{:S(2)}, u32[]{:S(2)}) collective-permute-start(f32[4,1024]{1,0:T(4,128)} %refs_0_.2), channel_id=1, source_target_pairs={{0,1},{1,0},{2,3},{3,2},{4,5},{5,4},{6,7},{7,6},{8,9},{9,8},{10,11... | collective-permute-start | bytes 49160 | tf_op jit(solution)/shard_map/ppermute | solution.py:340
  6.3 5.7 %collective-permute-start.2 = (f32[4,1024]{1,0:T(4,128)}, f32[4,1024]{1,0:T(4,128)S(1)}, u32[]{:S(2)}, u32[]{:S(2)}) collective-permute-start(f32[4,1024]{1,0:T(4,128)} %refs_0_.2), channel_id=1, source_target_pairs={{0,3},{1,2},{2,1},{3,0},{4,7},{5,6},{6,5},{7,4},{8,11},{9,10},{10,... | collective-permute-start | bytes 49160 | tf_op jit(solution)/shard_map/ppermute | solution.py:340
  6.3 0.8 %copy-start.4 = (f32[4,1024]{1,0:T(4,128)S(1)}, f32[4,1024]{1,0:T(4,128)}, u32[]{:S(2)}) copy-start(f32[4,1024]{1,0:T(4,128)} %refs_0_.2) | copy-start | bytes 49156
  7.4 11.5 %copy-start = (bf16[256,2048]{1,0:T(8,128)(2,1)S(1)}, bf16[256,2048]{1,0:T(8,128)(2,1)}, u32[]{:S(2)}) copy-start(bf16[256,2048]{1,0:T(8,128)(2,1)} %q_ref.3) | copy-start | bytes 3145732
  7.5 11.5 %copy-start.1 = (bf16[256,2048]{1,0:T(8,128)(2,1)S(1)}, bf16[256,2048]{1,0:T(8,128)(2,1)}, u32[]{:S(2)}) copy-start(bf16[256,2048]{1,0:T(8,128)(2,1)} %k_ref.3) | copy-start | bytes 3145732
  7.5 11.5 %copy-start.2 = (bf16[256,2048]{1,0:T(8,128)(2,1)S(1)}, bf16[256,2048]{1,0:T(8,128)(2,1)}, u32[]{:S(2)}) copy-start(bf16[256,2048]{1,0:T(8,128)(2,1)} %v_ref.3) | copy-start | bytes 3145732
  7.5 11.5 %copy-start.3 = (bf16[256,2048]{1,0:T(8,128)(2,1)S(1)}, bf16[256,2048]{1,0:T(8,128)(2,1)}, u32[]{:S(2)}) copy-start(bf16[256,2048]{1,0:T(8,128)(2,1)} %g_ref.3) | copy-start | bytes 3145732
  14.5 6.4 %collective-permute-start.13 = (bf16[2,2,128,128]{3,2,1,0:T(8,128)(2,1)S(1)}, bf16[2,2,128,128]{3,2,1,0:T(8,128)(2,1)S(1)}, u32[]{:S(2)}, u32[]{:S(2)}) collective-permute-start(bf16[2,2,128,128]{3,2,1,0:T(8,128)(2,1)S(1)} %get-tuple-element.74), channel_id=1, source_target_pairs={{0,1},{1,0},{2,3},{3,2},{4,5},{5,4},{6,7},{7,6},{8,9},{9,8},{10,11... | collective-permute-start | bytes 393224 | tf_op jit(solution)/shard_map/ppermute | solution.py:340
  14.6 17.5 %collective-permute-start.14 = (bf16[2,2,128,128]{3,2,1,0:T(8,128)(2,1)S(1)}, bf16[2,2,128,128]{3,2,1,0:T(8,128)(2,1)S(1)}, u32[]{:S(2)}, u32[]{:S(2)}) collective-permute-start(bf16[2,2,128,128]{3,2,1,0:T(8,128)(2,1)S(1)} %get-tuple-element.75), channel_id=1, source_target_pairs={{0,2},{1,3},{2,0},{3,1},{4,6},{5,7},{6,4},{7,5},{8,10},{9,11},{10,... | collective-permute-start | bytes 393224 | tf_op jit(solution)/shard_map/ppermute | solution.py:340
  15.5 16.6 %collective-permute-start.15 = (bf16[2,2,128,128]{3,2,1,0:T(8,128)(2,1)S(1)}, bf16[2,2,128,128]{3,2,1,0:T(8,128)(2,1)S(1)}, u32[]{:S(2)}, u32[]{:S(2)}) collective-permute-start(bf16[2,2,128,128]{3,2,1,0:T(8,128)(2,1)S(1)} %get-tuple-element.76), channel_id=1, source_target_pairs={{0,3},{1,2},{2,1},{3,0},{4,7},{5,6},{6,5},{7,4},{8,11},{9,10},{10,... | collective-permute-start | bytes 393224 | tf_op jit(solution)/shard_map/ppermute | solution.py:340
  19.8 12.5 %collective-permute-start.3 = (bf16[2,2,128,128]{3,2,1,0:T(8,128)(2,1)S(1)}, bf16[2,2,128,128]{3,2,1,0:T(8,128)(2,1)S(1)}, u32[]{:S(2)}, u32[]{:S(2)}) collective-permute-start(bf16[2,2,128,128]{3,2,1,0:T(8,128)(2,1)S(1)} %get-tuple-element.54), channel_id=1, source_target_pairs={{0,1},{1,0},{2,3},{3,2},{4,5},{5,4},{6,7},{7,6},{8,9},{9,8},{10,11... | collective-permute-start | bytes 393224 | tf_op jit(solution)/shard_map/ppermute | solution.py:340
  19.9 17.6 %collective-permute-start.4 = (bf16[2,2,128,128]{3,2,1,0:T(8,128)(2,1)S(1)}, bf16[2,2,128,128]{3,2,1,0:T(8,128)(2,1)S(1)}, u32[]{:S(2)}, u32[]{:S(2)}) collective-permute-start(bf16[2,2,128,128]{3,2,1,0:T(8,128)(2,1)S(1)} %get-tuple-element.55), channel_id=1, source_target_pairs={{0,2},{1,3},{2,0},{3,1},{4,6},{5,7},{6,4},{7,5},{8,10},{9,11},{10,... | collective-permute-start | bytes 393224 | tf_op jit(solution)/shard_map/ppermute | solution.py:340
  20.9 16.5 %collective-permute-start.5 = (bf16[2,2,128,128]{3,2,1,0:T(8,128)(2,1)S(1)}, bf16[2,2,128,128]{3,2,1,0:T(8,128)(2,1)S(1)}, u32[]{:S(2)}, u32[]{:S(2)}) collective-permute-start(bf16[2,2,128,128]{3,2,1,0:T(8,128)(2,1)S(1)} %get-tuple-element.56), channel_id=1, source_target_pairs={{0,3},{1,2},{2,1},{3,0},{4,7},{5,6},{6,5},{7,4},{8,11},{9,10},{10,... | collective-permute-start | bytes 393224 | tf_op jit(solution)/shard_map/ppermute | solution.py:340
  32.2 5.4 %collective-permute-start.16 = (bf16[528,128]{1,0:T(8,128)(2,1)S(1)}, bf16[528,128]{1,0:T(8,128)(2,1)S(1)}, u32[]{:S(2)}, u32[]{:S(2)}) collective-permute-start(bf16[528,128]{1,0:T(8,128)(2,1)S(1)} %shard_map.89.own_ref), channel_id=1, source_target_pairs={{0,4},{4,0},{8,12},{12,8},{16,20},{20,16},{24,28},{28,24},{1,5},{5... | collective-permute-start | bytes 405512 | tf_op jit(solution)/shard_map/ppermute | solution.py:340
  37.6 10.9 %collective-permute-start.6 = (bf16[528,128]{1,0:T(8,128)(2,1)S(1)}, bf16[528,128]{1,0:T(8,128)(2,1)S(1)}, u32[]{:S(2)}, u32[]{:S(2)}) collective-permute-start(bf16[528,128]{1,0:T(8,128)(2,1)S(1)} %shard_map.85.own_ref), channel_id=1, source_target_pairs={{0,4},{4,0},{8,12},{12,8},{16,20},{20,16},{24,28},{28,24},{1,5},{5... | collective-permute-start | bytes 405512 | tf_op jit(solution)/shard_map/ppermute | solution.py:340
  37.8 4.6 %collective-permute-start.17 = (bf16[272,128]{1,0:T(8,128)(2,1)S(1)}, bf16[272,128]{1,0:T(8,128)(2,1)S(1)}, u32[]{:S(2)}, u32[]{:S(2)}) collective-permute-start(bf16[272,128]{1,0:T(8,128)(2,1)S(1)} %get-tuple-element.77), channel_id=1, source_target_pairs={{0,8},{4,12},{8,0},{12,4},{16,24},{20,28},{24,16},{28,20},{1,9},{5... | collective-permute-start | bytes 208904 | tf_op jit(solution)/shard_map/ppermute | solution.py:340
  39.3 4.3 %collective-permute-start.18 = (bf16[272,128]{1,0:T(8,128)(2,1)S(1)}, bf16[272,128]{1,0:T(8,128)(2,1)S(1)}, u32[]{:S(2)}, u32[]{:S(2)}) collective-permute-start(bf16[272,128]{1,0:T(8,128)(2,1)S(1)} %get-tuple-element.78), channel_id=1, source_target_pairs={{0,16},{4,20},{8,24},{12,28},{16,0},{20,4},{24,8},{28,12},{1,17},{... | collective-permute-start | bytes 208904 | tf_op jit(solution)/shard_map/ppermute | solution.py:340
  40.8 5.2 %collective-permute-start.19 = (bf16[272,128]{1,0:T(8,128)(2,1)S(1)}, bf16[272,128]{1,0:T(8,128)(2,1)S(1)}, u32[]{:S(2)}, u32[]{:S(2)}) collective-permute-start(bf16[272,128]{1,0:T(8,128)(2,1)S(1)} %get-tuple-element.79), channel_id=1, source_target_pairs={{0,24},{4,28},{8,16},{12,20},{16,8},{20,12},{24,0},{28,4},{1,25},{... | collective-permute-start | bytes 208904 | tf_op jit(solution)/shard_map/ppermute | solution.py:340
  46.4 11.4 %collective-permute-start.20 = (bf16[2,2,128,128]{3,2,1,0:T(8,128)(2,1)S(1)}, bf16[2,2,128,128]{3,2,1,0:T(8,128)(2,1)S(1)}, u32[]{:S(2)}, u32[]{:S(2)}) collective-permute-start(bf16[2,2,128,128]{3,2,1,0:T(8,128)(2,1)S(1)} %get-tuple-element.81), channel_id=1, source_target_pairs={{0,1},{1,0},{2,3},{3,2},{4,5},{5,4},{6,7},{7,6},{8,9},{9,8},{10,11... | collective-permute-start | bytes 393224 | tf_op jit(solution)/shard_map/ppermute | solution.py:340
  48.6 4.4 %collective-permute-start.7 = (bf16[272,128]{1,0:T(8,128)(2,1)S(1)}, bf16[272,128]{1,0:T(8,128)(2,1)S(1)}, u32[]{:S(2)}, u32[]{:S(2)}) collective-permute-start(bf16[272,128]{1,0:T(8,128)(2,1)S(1)} %get-tuple-element.57), channel_id=1, source_target_pairs={{0,8},{4,12},{8,0},{12,4},{16,24},{20,28},{24,16},{28,20},{1,9},{5... | collective-permute-start | bytes 208904 | tf_op jit(solution)/shard_map/ppermute | solution.py:340
  49.2 5.4 %collective-permute-start.8 = (bf16[272,128]{1,0:T(8,128)(2,1)S(1)}, bf16[272,128]{1,0:T(8,128)(2,1)S(1)}, u32[]{:S(2)}, u32[]{:S(2)}) collective-permute-start(bf16[272,128]{1,0:T(8,128)(2,1)S(1)} %get-tuple-element.58), channel_id=1, source_target_pairs={{0,16},{4,20},{8,24},{12,28},{16,0},{20,4},{24,8},{28,12},{1,17},{... | collective-permute-start | bytes 208904 | tf_op jit(solution)/shard_map/ppermute | solution.py:340
  49.8 5.2 %collective-permute-start.9 = (bf16[272,128]{1,0:T(8,128)(2,1)S(1)}, bf16[272,128]{1,0:T(8,128)(2,1)S(1)}, u32[]{:S(2)}, u32[]{:S(2)}) collective-permute-start(bf16[272,128]{1,0:T(8,128)(2,1)S(1)} %get-tuple-element.59), channel_id=1, source_target_pairs={{0,24},{4,28},{8,16},{12,20},{16,8},{20,12},{24,0},{28,4},{1,25},{... | collective-permute-start | bytes 208904 | tf_op jit(solution)/shard_map/ppermute | solution.py:340
  52.1 15.6 %collective-permute-start.21 = (bf16[2,2,128,128]{3,2,1,0:T(8,128)(2,1)S(1)}, bf16[2,2,128,128]{3,2,1,0:T(8,128)(2,1)S(1)}, u32[]{:S(2)}, u32[]{:S(2)}) collective-permute-start(bf16[2,2,128,128]{3,2,1,0:T(8,128)(2,1)S(1)} %get-tuple-element.82), channel_id=1, source_target_pairs={{0,2},{1,3},{2,0},{3,1},{4,6},{5,7},{6,4},{7,5},{8,10},{9,11},{10,... | collective-permute-start | bytes 393224 | tf_op jit(solution)/shard_map/ppermute | solution.py:340
  53.0 14.8 %collective-permute-start.22 = (bf16[2,2,128,128]{3,2,1,0:T(8,128)(2,1)S(1)}, bf16[2,2,128,128]{3,2,1,0:T(8,128)(2,1)S(1)}, u32[]{:S(2)}, u32[]{:S(2)}) collective-permute-start(bf16[2,2,128,128]{3,2,1,0:T(8,128)(2,1)S(1)} %get-tuple-element.83), channel_id=1, source_target_pairs={{0,3},{1,2},{2,1},{3,0},{4,7},{5,6},{6,5},{7,4},{8,11},{9,10},{10,... | collective-permute-start | bytes 393224 | tf_op jit(solution)/shard_map/ppermute | solution.py:340
  55.4 15.3 %collective-permute-start.10 = (bf16[2,2,128,128]{3,2,1,0:T(8,128)(2,1)S(1)}, bf16[2,2,128,128]{3,2,1,0:T(8,128)(2,1)S(1)}, u32[]{:S(2)}, u32[]{:S(2)}) collective-permute-start(bf16[2,2,128,128]{3,2,1,0:T(8,128)(2,1)S(1)} %get-tuple-element.60), channel_id=1, source_target_pairs={{0,1},{1,0},{2,3},{3,2},{4,5},{5,4},{6,7},{7,6},{8,9},{9,8},{10,11... | collective-permute-start | bytes 393224 | tf_op jit(solution)/shard_map/ppermute | solution.py:340
  56.1 17.2 %collective-permute-start.11 = (bf16[2,2,128,128]{3,2,1,0:T(8,128)(2,1)S(1)}, bf16[2,2,128,128]{3,2,1,0:T(8,128)(2,1)S(1)}, u32[]{:S(2)}, u32[]{:S(2)}) collective-permute-start(bf16[2,2,128,128]{3,2,1,0:T(8,128)(2,1)S(1)} %get-tuple-element.61), channel_id=1, source_target_pairs={{0,2},{1,3},{2,0},{3,1},{4,6},{5,7},{6,4},{7,5},{8,10},{9,11},{10,... | collective-permute-start | bytes 393224 | tf_op jit(solution)/shard_map/ppermute | solution.py:340
  57.8 15.5 %collective-permute-start.12 = (bf16[2,2,128,128]{3,2,1,0:T(8,128)(2,1)S(1)}, bf16[2,2,128,128]{3,2,1,0:T(8,128)(2,1)S(1)}, u32[]{:S(2)}, u32[]{:S(2)}) collective-permute-start(bf16[2,2,128,128]{3,2,1,0:T(8,128)(2,1)S(1)} %get-tuple-element.62), channel_id=1, source_target_pairs={{0,3},{1,2},{2,1},{3,0},{4,7},{5,6},{6,5},{7,4},{8,11},{9,10},{10,... | collective-permute-start | bytes 393224 | tf_op jit(solution)/shard_map/ppermute | solution.py:340
where the time goes:
time: 75.1 us; the launch traced here: 74.9 us
  starting transfers between devices  29.8 us (40%)
  waiting for transfers between devices  28.1 us (37%)
  Pallas kernels  15.4 us (21%)
  local copies, waits for them, and re-layouts  0.81 us (1%)
  between operations  0.81 us (1%)
    ppermute x23, starting transfers between devices, swap(): return lax.ppermute(array, axis, [(i, i ^ offset) for i in range(size)])  29.8 us
    ppermute x23, waiting for transfers between devices, swap(): return lax.ppermute(array, axis, [(i, i ^ offset) for i in range(size)])  28.1 us
    pallas_call x2, Pallas kernels, on_device(): parts = inner_call(rows, cols, *inputs)  6.05 us
    pallas_call x3, Pallas kernels, on_device(): pl.pallas_call(functools.partial(result_kernel, low=low, part=part, owner...  4.53 us
    pallas_call x1, Pallas kernels, on_device(): pl.pallas_call(functools.partial(first_kernel, part=part, owners=owners),...  2.43 us
  transfers between devices with their start and end apart: 23, of which 12 were waited for; matrix products, arithmetic and copies ran while one was open for 0% of the time, Pallas kernels for 15%

commit v1 on v0

--- a/solution.py
+++ b/solution.py
@@ -409,13 +409,14 @@
         )
         total = total_call(weights, *here)
         other = swap(total, SEQ, seq_size, 1)
-        sent = pl.pallas_call(
+        pair_call = pl.pallas_call(
             functools.partial(pair_kernel, part=part),
             out_shape=(far_shape,) * far,
             in_specs=[whole, whole],
             out_specs=(whole,) * far,
             compiler_params=params(),
-        )(total, other)
+        )
+        sent = pair_call(total, other)
         heard = [swap(array, SEQ, seq_size, PAIR * (slot + 1)) for slot, array in enumerate(sent)]
         state_call = pl.pallas_call(
             functools.partial(
@@ -437,7 +438,11 @@
             compiler_params=params(),
         )
         parts = inner_call(rows, cols, *inputs)
-        for slots in (range(1), range(1, owners)) if chunk == len(chunks) - 1 else (range(owners),):
+        groups = [range(owners)]
+        if chunk == len(chunks) - 1:
+            half = owners // 2
+            groups = [(0,), (half,), [slot for slot in range(1, owners) if slot != half]]
+        for slots in groups:
             carried = 0 if outs is None else 4
             first_carried = 8 + len(slots)
             outs = pl.pallas_call(

time: 75.1 us -> 73.9 us (0.984)
  waiting for transfers between devices: 28.1 us -> 25 us
  Pallas kernels: 15.4 us -> 16.4 us
  starting transfers between devices: 29.8 us -> 30.7 us
    ppermute x23, waiting for transfers between devices: 28.1 us -> 25 us  [swap(): return lax.ppermute(array, axis, [(i, i ^ offset) for i in range(size)])]
    pallas_call x3 -> x4, Pallas kernels: 4.53 us -> 5.58 us  [on_device(): pl.pallas_call(functools.partial(result_kernel, low=low, part=part, owner...]
    ppermute x23, starting transfers between devices: 29.8 us -> 30.7 us  [swap(): return lax.ppermute(array, axis, [(i, i ^ offset) for i in range(size)])]
  transfers between devices with their start and end apart: 23 -> 23, of which waited for: 12 -> 8; matrix products, arithmetic and copies ran while one was open for 0% -> 0% of each run, Pallas kernels for 15% -> 17%
where the time goes in v1:
time: 73.9 us; the launch traced here: 73.7 us
  starting transfers between devices  30.7 us (42%)
  waiting for transfers between devices  25 us (34%)
  Pallas kernels  16.4 us (22%)
  between operations  0.83 us (1%)
  local copies, waits for them, and re-layouts  0.81 us (1%)
    ppermute x23, starting transfers between devices, swap(): return lax.ppermute(array, axis, [(i, i ^ offset) for i in range(size)])  30.7 us
    ppermute x23, waiting for transfers between devices, swap(): return lax.ppermute(array, axis, [(i, i ^ offset) for i in range(size)])  25 us
    pallas_call x2, Pallas kernels, on_device(): parts = inner_call(rows, cols, *inputs)  6.04 us
    pallas_call x4, Pallas kernels, on_device(): pl.pallas_call(functools.partial(result_kernel, low=low, part=part, owner...  5.58 us
    pallas_call x1, Pallas kernels, on_device(): pl.pallas_call(functools.partial(first_kernel, part=part, owners=owners),...  2.43 us
  transfers between devices with their start and end apart: 23, of which 8 were waited for; matrix products, arithmetic and copies ran while one was open for 0% of the time, Pallas kernels for 17%

profile of v1, /device:TPU:0, one launch (start us, length us, event | category | flops | bytes accessed | tf_op | source)
XLA Modules:
  0.0 73.7 jit_solution(16452524304569552851)
XLA Ops:
  0.6 4.1 %collective-permute-start.1 = (f32[4,1024]{1,0:T(4,128)}, f32[4,1024]{1,0:T(4,128)S(1)}, u32[]{:S(2)}, u32[]{:S(2)}) collective-permute-start(f32[4,1024]{1,0:T(4,128)} %refs_0_.2), channel_id=1, source_target_pairs={{0,2},{1,3},{2,0},{3,1},{4,6},{5,7},{6,4},{7,5},{8,10},{9,11},{10,... | collective-permute-start | bytes 49160 | tf_op jit(solution)/shard_map/ppermute | solution.py:340
  4.8 1.6 %collective-permute-start = (f32[4,1024]{1,0:T(4,128)}, f32[4,1024]{1,0:T(4,128)S(1)}, u32[]{:S(2)}, u32[]{:S(2)}) collective-permute-start(f32[4,1024]{1,0:T(4,128)} %refs_0_.2), channel_id=1, source_target_pairs={{0,1},{1,0},{2,3},{3,2},{4,5},{5,4},{6,7},{7,6},{8,9},{9,8},{10,11... | collective-permute-start | bytes 49160 | tf_op jit(solution)/shard_map/ppermute | solution.py:340
  6.3 0.0 collective-permute-start.2
  6.3 0.8 %copy-done.4 = f32[4,1024]{1,0:T(4,128)S(1)} copy-done((f32[4,1024]{1,0:T(4,128)S(1)}, f32[4,1024]{1,0:T(4,128)}, u32[]{:S(2)}) %copy-start.4) | copy-done | bytes 16408
  7.1 0.3 link.1._.w_ref
  7.4 0.0 copy-start
  7.5 0.0 copy-start.1
  7.5 0.0 copy-start.2
  7.5 0.0 copy-start.3
  7.5 0.0 collective-permute-done.1.refs_2_
  7.5 1.2 %collective-permute-done.refs_1_ = f32[4,1024]{1,0:T(4,128)S(1)} collective-permute-done((f32[4,1024]{1,0:T(4,128)}, f32[4,1024]{1,0:T(4,128)S(1)}, u32[]{:S(2)}, u32[]{:S(2)}) %collective-permute-start) | collective-permute-done | bytes 16416 | tf_op jit(solution)/shard_map/ppermute | solution.py:340
  8.7 3.4 %collective-permute-done.2.refs_3_ = f32[4,1024]{1,0:T(4,128)S(1)} collective-permute-done((f32[4,1024]{1,0:T(4,128)}, f32[4,1024]{1,0:T(4,128)S(1)}, u32[]{:S(2)}, u32[]{:S(2)}) %collective-permute-start.2) | collective-permute-done | bytes 16416 | tf_op jit(solution)/shard_map/ppermute | solution.py:340
  12.1 2.4 %first.1 = (f32[4,4,256]{2,1,0:T(4,128)S(1)}, f32[4,256,4]{2,1,0:T(8,128)S(1)}, bf16[2,2,128,128]{3,2,1,0:T(8,128)(2,1)S(1)}, bf16[2,2,128,128]{3,2,1,0:T(8,128)...) custom-call(f32[4,48,128]{2,1,0:T(8,128)S(1)} %link.1._.w_ref, ...), custom_call_target="tpu_custom_call" | custom-call | flops 134217728 | bytes 2097152 | tf_op jit(solution)/shard_map/first/pallas_call | solution.py:370
  14.5 0.1 collective-permute-start.13
  14.6 0.9 %collective-permute-start.14 = (bf16[2,2,128,128]{3,2,1,0:T(8,128)(2,1)S(1)}, bf16[2,2,128,128]{3,2,1,0:T(8,128)(2,1)S(1)}, u32[]{:S(2)}, u32[]{:S(2)}) collective-permute-start(bf16[2,2,128,128]{3,2,1,0:T(8,128)(2,1)S(1)} %get-tuple-element.79), channel_id=1, source_target_pairs={{0,2},{1,3},{2,0},{3,1},{4,6},{5,7},{6,4},{7,5},{8,10},{9,11},{10,... | collective-permute-start | bytes 393224 | tf_op jit(solution)/shard_map/ppermute | solution.py:340
  15.5 3.5 %collective-permute-start.15 = (bf16[2,2,128,128]{3,2,1,0:T(8,128)(2,1)S(1)}, bf16[2,2,128,128]{3,2,1,0:T(8,128)(2,1)S(1)}, u32[]{:S(2)}, u32[]{:S(2)}) collective-permute-start(bf16[2,2,128,128]{3,2,1,0:T(8,128)(2,1)S(1)} %get-tuple-element.80), channel_id=1, source_target_pairs={{0,3},{1,2},{2,1},{3,0},{4,7},{5,6},{6,5},{7,4},{8,11},{9,10},{10,... | collective-permute-start | bytes 393224 | tf_op jit(solution)/shard_map/ppermute | solution.py:340
  19.0 0.8 %shard_map.84 = (bf16[2,2,128,128]{3,2,1,0:T(8,128)(2,1)S(1)}, bf16[2,2,128,128]{3,2,1,0:T(8,128)(2,1)S(1)}, bf16[2,2,128,128]{3,2,1,0:T(8,128)(2,1)S(1)}, bf16[2,2,128,128]{3,2,1,0:T(8,128)(2,1)S(1)}) custom-call(f32[4,4,256]{2,1,0:T(4,128)S(1)} %get-tuple-element.56.row_ref, bf16[256,2048]{1,0:T(8,128)(2,1)S(1)} %copy-done, ...), custom_call_target="tpu_custom_call" | custom-call | flops 134217728 | bytes 2097152 | tf_op jit(solution)/shard_map/pallas_call | solution.py:393
  19.8 0.1 collective-permute-start.3
  19.9 0.9 %collective-permute-start.4 = (bf16[2,2,128,128]{3,2,1,0:T(8,128)(2,1)S(1)}, bf16[2,2,128,128]{3,2,1,0:T(8,128)(2,1)S(1)}, u32[]{:S(2)}, u32[]{:S(2)}) collective-permute-start(bf16[2,2,128,128]{3,2,1,0:T(8,128)(2,1)S(1)} %get-tuple-element.59), channel_id=1, source_target_pairs={{0,2},{1,3},{2,0},{3,1},{4,6},{5,7},{6,4},{7,5},{8,10},{9,11},{10,... | collective-permute-start | bytes 393224 | tf_op jit(solution)/shard_map/ppermute | solution.py:340
  20.8 0.1 collective-permute-done.13.refs_1_
  20.9 3.3 %collective-permute-start.5 = (bf16[2,2,128,128]{3,2,1,0:T(8,128)(2,1)S(1)}, bf16[2,2,128,128]{3,2,1,0:T(8,128)(2,1)S(1)}, u32[]{:S(2)}, u32[]{:S(2)}) collective-permute-start(bf16[2,2,128,128]{3,2,1,0:T(8,128)(2,1)S(1)} %get-tuple-element.60), channel_id=1, source_target_pairs={{0,3},{1,2},{2,1},{3,0},{4,7},{5,6},{6,5},{7,4},{8,11},{9,10},{10,... | collective-permute-start | bytes 393224 | tf_op jit(solution)/shard_map/ppermute | solution.py:340
  24.3 7.8 %collective-permute-done.14.refs_2_ = bf16[2,2,128,128]{3,2,1,0:T(8,128)(2,1)S(1)} collective-permute-done((bf16[2,2,128,128]{3,2,1,0:T(8,128)(2,1)S(1)}, bf16[2,2,128,128]{3,2,1,0:T(8,128)(2,1)S(1)}, u32[]{:S(2)}, u32[]{:S(2)}) %collective-permute-start.14) | collective-permute-done | bytes 131104 | tf_op jit(solution)/shard_map/ppermute | solution.py:340
  32.1 0.0 collective-permute-done.15.refs_3_
  32.1 0.1 shard_map.89.own_ref
  32.2 0.1 collective-permute-start.16
  32.3 0.0 collective-permute-done.3.refs_1_
  32.3 5.2 %collective-permute-done.4.refs_2_ = bf16[2,2,128,128]{3,2,1,0:T(8,128)(2,1)S(1)} collective-permute-done((bf16[2,2,128,128]{3,2,1,0:T(8,128)(2,1)S(1)}, bf16[2,2,128,128]{3,2,1,0:T(8,128)(2,1)S(1)}, u32[]{:S(2)}, u32[]{:S(2)}) %collective-permute-start.4) | collective-permute-done | bytes 131104 | tf_op jit(solution)/shard_map/ppermute | solution.py:340
  37.4 0.0 collective-permute-done.5.refs_3_
  37.4 0.1 shard_map.85.own_ref
  37.6 0.1 collective-permute-start.6
  37.6 0.0 collective-permute-done.16.other_ref.refs_4_
  37.6 0.1 shard_map.90
  37.8 1.6 %collective-permute-start.17 = (bf16[272,128]{1,0:T(8,128)(2,1)S(1)}, bf16[272,128]{1,0:T(8,128)(2,1)S(1)}, u32[]{:S(2)}, u32[]{:S(2)}) collective-permute-start(bf16[272,128]{1,0:T(8,128)(2,1)S(1)} %get-tuple-element.81), channel_id=1, source_target_pairs={{0,8},{4,12},{8,0},{12,4},{16,24},{20,28},{24,16},{28,20},{1,9},{5... | collective-permute-start | bytes 208904 | tf_op jit(solution)/shard_map/ppermute | solution.py:340
  39.3 1.5 %collective-permute-start.18 = (bf16[272,128]{1,0:T(8,128)(2,1)S(1)}, bf16[272,128]{1,0:T(8,128)(2,1)S(1)}, u32[]{:S(2)}, u32[]{:S(2)}) collective-permute-start(bf16[272,128]{1,0:T(8,128)(2,1)S(1)} %get-tuple-element.82), channel_id=1, source_target_pairs={{0,16},{4,20},{8,24},{12,28},{16,0},{20,4},{24,8},{28,12},{1,17},{... | collective-permute-start | bytes 208904 | tf_op jit(solution)/shard_map/ppermute | solution.py:340
  40.8 0.5 collective-permute-start.19
  41.3 0.0 collective-permute-done.6.other_ref.refs_4_
  41.3 0.1 shard_map.86
  41.4 1.6 %collective-permute-start.7 = (bf16[272,128]{1,0:T(8,128)(2,1)S(1)}, bf16[272,128]{1,0:T(8,128)(2,1)S(1)}, u32[]{:S(2)}, u32[]{:S(2)}) collective-permute-start(bf16[272,128]{1,0:T(8,128)(2,1)S(1)} %get-tuple-element.61), channel_id=1, source_target_pairs={{0,8},{4,12},{8,0},{12,4},{16,24},{20,28},{24,16},{28,20},{1,9},{5... | collective-permute-start | bytes 208904 | tf_op jit(solution)/shard_map/ppermute | solution.py:340
  43.0 1.5 %collective-permute-start.8 = (bf16[272,128]{1,0:T(8,128)(2,1)S(1)}, bf16[272,128]{1,0:T(8,128)(2,1)S(1)}, u32[]{:S(2)}, u32[]{:S(2)}) collective-permute-start(bf16[272,128]{1,0:T(8,128)(2,1)S(1)} %get-tuple-element.62), channel_id=1, source_target_pairs={{0,16},{4,20},{8,24},{12,28},{16,0},{20,4},{24,8},{28,12},{1,17},{... | collective-permute-start | bytes 208904 | tf_op jit(solution)/shard_map/ppermute | solution.py:340
  44.5 0.0 collective-permute-done.17.refs_5_
  44.5 0.5 collective-permute-start.9
  45.0 0.0 collective-permute-done.18.refs_6_
  45.0 1.5 %collective-permute-done.19.refs_7_ = bf16[272,128]{1,0:T(8,128)(2,1)S(1)} collective-permute-done((bf16[272,128]{1,0:T(8,128)(2,1)S(1)}, bf16[272,128]{1,0:T(8,128)(2,1)S(1)}, u32[]{:S(2)}, u32[]{:S(2)}) %collective-permute-start.19) | collective-permute-done | bytes 69664 | tf_op jit(solution)/shard_map/ppermute | solution.py:340
  46.5 0.4 shard_map.91
  46.9 2.0 %collective-permute-start.20 = (bf16[2,2,128,128]{3,2,1,0:T(8,128)(2,1)S(1)}, bf16[2,2,128,128]{3,2,1,0:T(8,128)(2,1)S(1)}, u32[]{:S(2)}, u32[]{:S(2)}) collective-permute-start(bf16[2,2,128,128]{3,2,1,0:T(8,128)(2,1)S(1)} %get-tuple-element.85), channel_id=1, source_target_pairs={{0,1},{1,0},{2,3},{3,2},{4,5},{5,4},{6,7},{7,6},{8,9},{9,8},{10,11... | collective-permute-start | bytes 393224 | tf_op jit(solution)/shard_map/ppermute | solution.py:340
  48.9 0.0 collective-permute-start.21
  48.9 0.0 collective-permute-done.7.refs_5_
  48.9 2.4 %collective-permute-start.22 = (bf16[2,2,128,128]{3,2,1,0:T(8,128)(2,1)S(1)}, bf16[2,2,128,128]{3,2,1,0:T(8,128)(2,1)S(1)}, u32[]{:S(2)}, u32[]{:S(2)}) collective-permute-start(bf16[2,2,128,128]{3,2,1,0:T(8,128)(2,1)S(1)} %get-tuple-element.87), channel_id=1, source_target_pairs={{0,3},{1,2},{2,1},{3,0},{4,7},{5,6},{6,5},{7,4},{8,11},{9,10},{10,... | collective-permute-start | bytes 393224 | tf_op jit(solution)/shard_map/ppermute | solution.py:340
  51.4 0.0 collective-permute-done.8.refs_6_
  51.4 0.0 collective-permute-done.9.refs_7_
  51.4 0.4 shard_map.87
  51.8 0.9 %collective-permute-start.12 = (bf16[2,2,128,128]{3,2,1,0:T(8,128)(2,1)S(1)}, bf16[2,2,128,128]{3,2,1,0:T(8,128)(2,1)S(1)}, u32[]{:S(2)}, u32[]{:S(2)}) collective-permute-start(bf16[2,2,128,128]{3,2,1,0:T(8,128)(2,1)S(1)} %get-tuple-element.75), channel_id=1, source_target_pairs={{0,2},{1,3},{2,0},{3,1},{4,6},{5,7},{6,4},{7,5},{8,10},{9,11},{10,... | collective-permute-start | bytes 393224 | tf_op jit(solution)/shard_map/ppermute | solution.py:340
  52.7 3.0 %shard_map.92 = (f32[4,256,256]{2,1,0:T(8,128)S(1)}, f32[4,256,256]{2,1,0:T(8,128)S(1)}, f32[4,256,256]{2,1,0:T(8,128)S(1)}, f32[4,256,256]{2,1,0:T(8,128)S(1)},...) custom-call(f32[4,4,256]{2,1,0:T(4,128)S(1)} %get-tuple-element.56.r, ...), custom_call_target="tpu_custom_call" | custom-call | flops 805306368 | bytes 6291456 | tf_op jit(solution)/shard_map/pallas_call | solution.py:440
  55.7 1.1 %collective-permute-start.10 = (bf16[2,2,128,128]{3,2,1,0:T(8,128)(2,1)S(1)}, bf16[2,2,128,128]{3,2,1,0:T(8,128)(2,1)S(1)}, u32[]{:S(2)}, u32[]{:S(2)}) collective-permute-start(bf16[2,2,128,128]{3,2,1,0:T(8,128)(2,1)S(1)} %get-tuple-element.64), channel_id=1, source_target_pairs={{0,1},{1,0},{2,3},{3,2},{4,5},{5,4},{6,7},{7,6},{8,9},{9,8},{10,11... | collective-permute-start | bytes 393224 | tf_op jit(solution)/shard_map/ppermute | solution.py:340
  56.9 2.4 %collective-permute-start.11 = (bf16[2,2,128,128]{3,2,1,0:T(8,128)(2,1)S(1)}, bf16[2,2,128,128]{3,2,1,0:T(8,128)(2,1)S(1)}, u32[]{:S(2)}, u32[]{:S(2)}) collective-permute-start(bf16[2,2,128,128]{3,2,1,0:T(8,128)(2,1)S(1)} %get-tuple-element.65), channel_id=1, source_target_pairs={{0,3},{1,2},{2,1},{3,0},{4,7},{5,6},{6,5},{7,4},{8,11},{9,10},{10,... | collective-permute-start | bytes 393224 | tf_op jit(solution)/shard_map/ppermute | solution.py:340
  59.3 3.0 %shard_map.88 = (f32[4,256,256]{2,1,0:T(8,128)S(1)}, f32[4,256,256]{2,1,0:T(8,128)S(1)}, f32[4,256,256]{2,1,0:T(8,128)S(1)}, f32[4,256,256]{2,1,0:T(8,128)S(1)},...) custom-call(f32[4,4,256]{2,1,0:T(4,128)S(1)} %get-tuple-element.56.r, ...), custom_call_target="tpu_custom_call" | custom-call | flops 805306368 | bytes 6291456 | tf_op jit(solution)/shard_map/pallas_call | solution.py:440
  62.4 1.7 %collective-permute-done.21.refs_2_ = bf16[2,2,128,128]{3,2,1,0:T(8,128)(2,1)S(1)} collective-permute-done((bf16[2,2,128,128]{3,2,1,0:T(8,128)(2,1)S(1)}, bf16[2,2,128,128]{3,2,1,0:T(8,128)(2,1)S(1)}, u32[]{:S(2)}, u32[]{:S(2)}) %collective-permute-start.21) | collective-permute-done | bytes 131104 | tf_op jit(solution)/shard_map/ppermute | solution.py:340
  64.0 0.0 collective-permute-done.22.refs_3_
  64.0 1.7 %shard_map.93 = (bf16[256,2048]{1,0:T(8,128)(2,1)}, bf16[256,2048]{1,0:T(8,128)(2,1)}, bf16[256,2048]{1,0:T(8,128)(2,1)}, bf16[256,2048]{1,0:T(8,128)(2,1)}) custom-call(bf16[2,2,128,128]{3,2,1,0:T(8,128)(2,1)S(1)} %get-tuple-element.84.refs_0_, bf16[2,2,128,128]{3,2,1,0:T(8,128)(2,1)S(1)} %collective-permute-done.20.refs_1_, ...), custom_call_target="tpu_custom_call" | custom-call | flops 268435456 | bytes 4194304 | tf_op jit(solution)/shard_map/pallas_call | solution.py:448
  65.8 1.2 %shard_map.94 = (bf16[256,2048]{1,0:T(8,128)(2,1)}, bf16[256,2048]{1,0:T(8,128)(2,1)}, bf16[256,2048]{1,0:T(8,128)(2,1)}, bf16[256,2048]{1,0:T(8,128)(2,1)}) custom-call(bf16[2,2,128,128]{3,2,1,0:T(8,128)(2,1)S(1)} %get-tuple-element.76.refs_0_, ...), custom_call_target="tpu_custom_call", output_to_operand_aliasing={{0}: (9, {}), {1}: (10, {}), {2}: (11, {}), {3}: (12, {})} | custom-call | flops 268435456 | bytes 4194304 | tf_op jit(solution)/shard_map/pallas_call | solution.py:448
  67.0 4.0 %collective-permute-done.12.refs_0_ = bf16[2,2,128,128]{3,2,1,0:T(8,128)(2,1)S(1)} collective-permute-done((bf16[2,2,128,128]{3,2,1,0:T(8,128)(2,1)S(1)}, bf16[2,2,128,128]{3,2,1,0:T(8,128)(2,1)S(1)}, u32[]{:S(2)}, u32[]{:S(2)}) %collective-permute-start.12) | collective-permute-done | bytes 131104 | tf_op jit(solution)/shard_map/ppermute | solution.py:340
  71.0 1.2 %shard_map.95 = (bf16[256,2048]{1,0:T(8,128)(2,1)}, bf16[256,2048]{1,0:T(8,128)(2,1)}, bf16[256,2048]{1,0:T(8,128)(2,1)}, bf16[256,2048]{1,0:T(8,128)(2,1)}) custom-call(bf16[2,2,128,128]{3,2,1,0:T(8,128)(2,1)S(1)} %collective-permute-done.12.refs_0_, ...), custom_call_target="tpu_custom_call", output_to_operand_aliasing={{0}: (9, {}), {1}: (10, {}), {2}: (11, {}), {3}: (12, {})} | custom-call | flops 268435456 | bytes 4194304 | tf_op jit(solution)/shard_map/pallas_call | solution.py:448
  72.3 0.0 collective-permute-done.11.refs_1_
  72.3 1.4 %shard_map.96 = (bf16[256,2048]{1,0:T(8,128)(2,1)}, bf16[256,2048]{1,0:T(8,128)(2,1)}, bf16[256,2048]{1,0:T(8,128)(2,1)}, bf16[256,2048]{1,0:T(8,128)(2,1)}) custom-call(bf16[2,2,128,128]{3,2,1,0:T(8,128)(2,1)S(1)} %collective-permute-done.10.refs_0_, ...), custom_call_target="tpu_custom_call", output_to_operand_aliasing={{0}: (10, {}), {1}: (11, {}), {2}: (12, {}), {3}: (13, {})} | custom-call | flops 268435456 | bytes 4194304 | tf_op jit(solution)/shard_map/pallas_call | solution.py:448
  (7 shorter events, 0.0 us)
Async XLA Ops:
  0.6 6.9 %collective-permute-start.1 = (f32[4,1024]{1,0:T(4,128)}, f32[4,1024]{1,0:T(4,128)S(1)}, u32[]{:S(2)}, u32[]{:S(2)}) collective-permute-start(f32[4,1024]{1,0:T(4,128)} %refs_0_.2), channel_id=1, source_target_pairs={{0,2},{1,3},{2,0},{3,1},{4,6},{5,7},{6,4},{7,5},{8,10},{9,11},{10,... | collective-permute-start | bytes 49160 | tf_op jit(solution)/shard_map/ppermute | solution.py:340
  4.8 3.9 %collective-permute-start = (f32[4,1024]{1,0:T(4,128)}, f32[4,1024]{1,0:T(4,128)S(1)}, u32[]{:S(2)}, u32[]{:S(2)}) collective-permute-start(f32[4,1024]{1,0:T(4,128)} %refs_0_.2), channel_id=1, source_target_pairs={{0,1},{1,0},{2,3},{3,2},{4,5},{5,4},{6,7},{7,6},{8,9},{9,8},{10,11... | collective-permute-start | bytes 49160 | tf_op jit(solution)/shard_map/ppermute | solution.py:340
  6.3 5.7 %collective-permute-start.2 = (f32[4,1024]{1,0:T(4,128)}, f32[4,1024]{1,0:T(4,128)S(1)}, u32[]{:S(2)}, u32[]{:S(2)}) collective-permute-start(f32[4,1024]{1,0:T(4,128)} %refs_0_.2), channel_id=1, source_target_pairs={{0,3},{1,2},{2,1},{3,0},{4,7},{5,6},{6,5},{7,4},{8,11},{9,10},{10,... | collective-permute-start | bytes 49160 | tf_op jit(solution)/shard_map/ppermute | solution.py:340
  6.3 0.8 %copy-start.4 = (f32[4,1024]{1,0:T(4,128)S(1)}, f32[4,1024]{1,0:T(4,128)}, u32[]{:S(2)}) copy-start(f32[4,1024]{1,0:T(4,128)} %refs_0_.2) | copy-start | bytes 49156
  7.4 11.5 %copy-start = (bf16[256,2048]{1,0:T(8,128)(2,1)S(1)}, bf16[256,2048]{1,0:T(8,128)(2,1)}, u32[]{:S(2)}) copy-start(bf16[256,2048]{1,0:T(8,128)(2,1)} %q_ref.3) | copy-start | bytes 3145732
  7.5 11.5 %copy-start.1 = (bf16[256,2048]{1,0:T(8,128)(2,1)S(1)}, bf16[256,2048]{1,0:T(8,128)(2,1)}, u32[]{:S(2)}) copy-start(bf16[256,2048]{1,0:T(8,128)(2,1)} %k_ref.3) | copy-start | bytes 3145732
  7.5 11.5 %copy-start.2 = (bf16[256,2048]{1,0:T(8,128)(2,1)S(1)}, bf16[256,2048]{1,0:T(8,128)(2,1)}, u32[]{:S(2)}) copy-start(bf16[256,2048]{1,0:T(8,128)(2,1)} %v_ref.3) | copy-start | bytes 3145732
  7.5 11.5 %copy-start.3 = (bf16[256,2048]{1,0:T(8,128)(2,1)S(1)}, bf16[256,2048]{1,0:T(8,128)(2,1)}, u32[]{:S(2)}) copy-start(bf16[256,2048]{1,0:T(8,128)(2,1)} %g_ref.3) | copy-start | bytes 3145732
  14.5 6.4 %collective-permute-start.13 = (bf16[2,2,128,128]{3,2,1,0:T(8,128)(2,1)S(1)}, bf16[2,2,128,128]{3,2,1,0:T(8,128)(2,1)S(1)}, u32[]{:S(2)}, u32[]{:S(2)}) collective-permute-start(bf16[2,2,128,128]{3,2,1,0:T(8,128)(2,1)S(1)} %get-tuple-element.78), channel_id=1, source_target_pairs={{0,1},{1,0},{2,3},{3,2},{4,5},{5,4},{6,7},{7,6},{8,9},{9,8},{10,11... | collective-permute-start | bytes 393224 | tf_op jit(solution)/shard_map/ppermute | solution.py:340
  14.6 17.5 %collective-permute-start.14 = (bf16[2,2,128,128]{3,2,1,0:T(8,128)(2,1)S(1)}, bf16[2,2,128,128]{3,2,1,0:T(8,128)(2,1)S(1)}, u32[]{:S(2)}, u32[]{:S(2)}) collective-permute-start(bf16[2,2,128,128]{3,2,1,0:T(8,128)(2,1)S(1)} %get-tuple-element.79), channel_id=1, source_target_pairs={{0,2},{1,3},{2,0},{3,1},{4,6},{5,7},{6,4},{7,5},{8,10},{9,11},{10,... | collective-permute-start | bytes 393224 | tf_op jit(solution)/shard_map/ppermute | solution.py:340
  15.5 16.6 %collective-permute-start.15 = (bf16[2,2,128,128]{3,2,1,0:T(8,128)(2,1)S(1)}, bf16[2,2,128,128]{3,2,1,0:T(8,128)(2,1)S(1)}, u32[]{:S(2)}, u32[]{:S(2)}) collective-permute-start(bf16[2,2,128,128]{3,2,1,0:T(8,128)(2,1)S(1)} %get-tuple-element.80), channel_id=1, source_target_pairs={{0,3},{1,2},{2,1},{3,0},{4,7},{5,6},{6,5},{7,4},{8,11},{9,10},{10,... | collective-permute-start | bytes 393224 | tf_op jit(solution)/shard_map/ppermute | solution.py:340
  19.8 12.5 %collective-permute-start.3 = (bf16[2,2,128,128]{3,2,1,0:T(8,128)(2,1)S(1)}, bf16[2,2,128,128]{3,2,1,0:T(8,128)(2,1)S(1)}, u32[]{:S(2)}, u32[]{:S(2)}) collective-permute-start(bf16[2,2,128,128]{3,2,1,0:T(8,128)(2,1)S(1)} %get-tuple-element.58), channel_id=1, source_target_pairs={{0,1},{1,0},{2,3},{3,2},{4,5},{5,4},{6,7},{7,6},{8,9},{9,8},{10,11... | collective-permute-start | bytes 393224 | tf_op jit(solution)/shard_map/ppermute | solution.py:340
  19.9 17.6 %collective-permute-start.4 = (bf16[2,2,128,128]{3,2,1,0:T(8,128)(2,1)S(1)}, bf16[2,2,128,128]{3,2,1,0:T(8,128)(2,1)S(1)}, u32[]{:S(2)}, u32[]{:S(2)}) collective-permute-start(bf16[2,2,128,128]{3,2,1,0:T(8,128)(2,1)S(1)} %get-tuple-element.59), channel_id=1, source_target_pairs={{0,2},{1,3},{2,0},{3,1},{4,6},{5,7},{6,4},{7,5},{8,10},{9,11},{10,... | collective-permute-start | bytes 393224 | tf_op jit(solution)/shard_map/ppermute | solution.py:340
  20.9 16.5 %collective-permute-start.5 = (bf16[2,2,128,128]{3,2,1,0:T(8,128)(2,1)S(1)}, bf16[2,2,128,128]{3,2,1,0:T(8,128)(2,1)S(1)}, u32[]{:S(2)}, u32[]{:S(2)}) collective-permute-start(bf16[2,2,128,128]{3,2,1,0:T(8,128)(2,1)S(1)} %get-tuple-element.60), channel_id=1, source_target_pairs={{0,3},{1,2},{2,1},{3,0},{4,7},{5,6},{6,5},{7,4},{8,11},{9,10},{10,... | collective-permute-start | bytes 393224 | tf_op jit(solution)/shard_map/ppermute | solution.py:340
  32.2 5.4 %collective-permute-start.16 = (bf16[528,128]{1,0:T(8,128)(2,1)S(1)}, bf16[528,128]{1,0:T(8,128)(2,1)S(1)}, u32[]{:S(2)}, u32[]{:S(2)}) collective-permute-start(bf16[528,128]{1,0:T(8,128)(2,1)S(1)} %shard_map.89.own_ref), channel_id=1, source_target_pairs={{0,4},{4,0},{8,12},{12,8},{16,20},{20,16},{24,28},{28,24},{1,5},{5... | collective-permute-start | bytes 405512 | tf_op jit(solution)/shard_map/ppermute | solution.py:340
  37.6 3.7 %collective-permute-start.6 = (bf16[528,128]{1,0:T(8,128)(2,1)S(1)}, bf16[528,128]{1,0:T(8,128)(2,1)S(1)}, u32[]{:S(2)}, u32[]{:S(2)}) collective-permute-start(bf16[528,128]{1,0:T(8,128)(2,1)S(1)} %shard_map.85.own_ref), channel_id=1, source_target_pairs={{0,4},{4,0},{8,12},{12,8},{16,20},{20,16},{24,28},{28,24},{1,5},{5... | collective-permute-start | bytes 405512 | tf_op jit(solution)/shard_map/ppermute | solution.py:340
  37.8 6.7 %collective-permute-start.17 = (bf16[272,128]{1,0:T(8,128)(2,1)S(1)}, bf16[272,128]{1,0:T(8,128)(2,1)S(1)}, u32[]{:S(2)}, u32[]{:S(2)}) collective-permute-start(bf16[272,128]{1,0:T(8,128)(2,1)S(1)} %get-tuple-element.81), channel_id=1, source_target_pairs={{0,8},{4,12},{8,0},{12,4},{16,24},{20,28},{24,16},{28,20},{1,9},{5... | collective-permute-start | bytes 208904 | tf_op jit(solution)/shard_map/ppermute | solution.py:340
  39.3 5.7 %collective-permute-start.18 = (bf16[272,128]{1,0:T(8,128)(2,1)S(1)}, bf16[272,128]{1,0:T(8,128)(2,1)S(1)}, u32[]{:S(2)}, u32[]{:S(2)}) collective-permute-start(bf16[272,128]{1,0:T(8,128)(2,1)S(1)} %get-tuple-element.82), channel_id=1, source_target_pairs={{0,16},{4,20},{8,24},{12,28},{16,0},{20,4},{24,8},{28,12},{1,17},{... | collective-permute-start | bytes 208904 | tf_op jit(solution)/shard_map/ppermute | solution.py:340
  40.8 5.7 %collective-permute-start.19 = (bf16[272,128]{1,0:T(8,128)(2,1)S(1)}, bf16[272,128]{1,0:T(8,128)(2,1)S(1)}, u32[]{:S(2)}, u32[]{:S(2)}) collective-permute-start(bf16[272,128]{1,0:T(8,128)(2,1)S(1)} %get-tuple-element.83), channel_id=1, source_target_pairs={{0,24},{4,28},{8,16},{12,20},{16,8},{20,12},{24,0},{28,4},{1,25},{... | collective-permute-start | bytes 208904 | tf_op jit(solution)/shard_map/ppermute | solution.py:340
  41.4 7.5 %collective-permute-start.7 = (bf16[272,128]{1,0:T(8,128)(2,1)S(1)}, bf16[272,128]{1,0:T(8,128)(2,1)S(1)}, u32[]{:S(2)}, u32[]{:S(2)}) collective-permute-start(bf16[272,128]{1,0:T(8,128)(2,1)S(1)} %get-tuple-element.61), channel_id=1, source_target_pairs={{0,8},{4,12},{8,0},{12,4},{16,24},{20,28},{24,16},{28,20},{1,9},{5... | collective-permute-start | bytes 208904 | tf_op jit(solution)/shard_map/ppermute | solution.py:340
  43.0 8.4 %collective-permute-start.8 = (bf16[272,128]{1,0:T(8,128)(2,1)S(1)}, bf16[272,128]{1,0:T(8,128)(2,1)S(1)}, u32[]{:S(2)}, u32[]{:S(2)}) collective-permute-start(bf16[272,128]{1,0:T(8,128)(2,1)S(1)} %get-tuple-element.62), channel_id=1, source_target_pairs={{0,16},{4,20},{8,24},{12,28},{16,0},{20,4},{24,8},{28,12},{1,17},{... | collective-permute-start | bytes 208904 | tf_op jit(solution)/shard_map/ppermute | solution.py:340
  44.5 6.9 %collective-permute-start.9 = (bf16[272,128]{1,0:T(8,128)(2,1)S(1)}, bf16[272,128]{1,0:T(8,128)(2,1)S(1)}, u32[]{:S(2)}, u32[]{:S(2)}) collective-permute-start(bf16[272,128]{1,0:T(8,128)(2,1)S(1)} %get-tuple-element.63), channel_id=1, source_target_pairs={{0,24},{4,28},{8,16},{12,20},{16,8},{20,12},{24,0},{28,4},{1,25},{... | collective-permute-start | bytes 208904 | tf_op jit(solution)/shard_map/ppermute | solution.py:340
  46.9 10.0 %collective-permute-start.20 = (bf16[2,2,128,128]{3,2,1,0:T(8,128)(2,1)S(1)}, bf16[2,2,128,128]{3,2,1,0:T(8,128)(2,1)S(1)}, u32[]{:S(2)}, u32[]{:S(2)}) collective-permute-start(bf16[2,2,128,128]{3,2,1,0:T(8,128)(2,1)S(1)} %get-tuple-element.85), channel_id=1, source_target_pairs={{0,1},{1,0},{2,3},{3,2},{4,5},{5,4},{6,7},{7,6},{8,9},{9,8},{10,11... | collective-permute-start | bytes 393224 | tf_op jit(solution)/shard_map/ppermute | solution.py:340
  48.9 15.1 %collective-permute-start.21 = (bf16[2,2,128,128]{3,2,1,0:T(8,128)(2,1)S(1)}, bf16[2,2,128,128]{3,2,1,0:T(8,128)(2,1)S(1)}, u32[]{:S(2)}, u32[]{:S(2)}) collective-permute-start(bf16[2,2,128,128]{3,2,1,0:T(8,128)(2,1)S(1)} %get-tuple-element.86), channel_id=1, source_target_pairs={{0,2},{1,3},{2,0},{3,1},{4,6},{5,7},{6,4},{7,5},{8,10},{9,11},{10,... | collective-permute-start | bytes 393224 | tf_op jit(solution)/shard_map/ppermute | solution.py:340
  48.9 15.1 %collective-permute-start.22 = (bf16[2,2,128,128]{3,2,1,0:T(8,128)(2,1)S(1)}, bf16[2,2,128,128]{3,2,1,0:T(8,128)(2,1)S(1)}, u32[]{:S(2)}, u32[]{:S(2)}) collective-permute-start(bf16[2,2,128,128]{3,2,1,0:T(8,128)(2,1)S(1)} %get-tuple-element.87), channel_id=1, source_target_pairs={{0,3},{1,2},{2,1},{3,0},{4,7},{5,6},{6,5},{7,4},{8,11},{9,10},{10,... | collective-permute-start | bytes 393224 | tf_op jit(solution)/shard_map/ppermute | solution.py:340
  51.8 19.3 %collective-permute-start.12 = (bf16[2,2,128,128]{3,2,1,0:T(8,128)(2,1)S(1)}, bf16[2,2,128,128]{3,2,1,0:T(8,128)(2,1)S(1)}, u32[]{:S(2)}, u32[]{:S(2)}) collective-permute-start(bf16[2,2,128,128]{3,2,1,0:T(8,128)(2,1)S(1)} %get-tuple-element.75), channel_id=1, source_target_pairs={{0,2},{1,3},{2,0},{3,1},{4,6},{5,7},{6,4},{7,5},{8,10},{9,11},{10,... | collective-permute-start | bytes 393224 | tf_op jit(solution)/shard_map/ppermute | solution.py:340
  55.7 16.5 %collective-permute-start.10 = (bf16[2,2,128,128]{3,2,1,0:T(8,128)(2,1)S(1)}, bf16[2,2,128,128]{3,2,1,0:T(8,128)(2,1)S(1)}, u32[]{:S(2)}, u32[]{:S(2)}) collective-permute-start(bf16[2,2,128,128]{3,2,1,0:T(8,128)(2,1)S(1)} %get-tuple-element.64), channel_id=1, source_target_pairs={{0,1},{1,0},{2,3},{3,2},{4,5},{5,4},{6,7},{7,6},{8,9},{9,8},{10,11... | collective-permute-start | bytes 393224 | tf_op jit(solution)/shard_map/ppermute | solution.py:340
  56.9 15.4 %collective-permute-start.11 = (bf16[2,2,128,128]{3,2,1,0:T(8,128)(2,1)S(1)}, bf16[2,2,128,128]{3,2,1,0:T(8,128)(2,1)S(1)}, u32[]{:S(2)}, u32[]{:S(2)}) collective-permute-start(bf16[2,2,128,128]{3,2,1,0:T(8,128)(2,1)S(1)} %get-tuple-element.65), channel_id=1, source_target_pairs={{0,3},{1,2},{2,1},{3,0},{4,7},{5,6},{6,5},{7,4},{8,11},{9,10},{10,... | collective-permute-start | bytes 393224 | tf_op jit(solution)/shard_map/ppermute | solution.py:340
